TPU v7x, 32 devices: a whole 2x2x4 slice. The times are simulated.
32 devices in a mesh: row: 4 (over y, x), col: 8 (over z, core).
Axes of the slice: x: 2, y: 2, z: 4, core: 2. Of those that a mesh axis runs over, the one named last changes fastest.
Arguments:
- tubes: bfloat16 [64, 1568, 1536], P(('row', 'col')), may hold values from -6 to 6
- tube_order: int32 [64, 1568], P(('row', 'col')), may hold values from 0 to 1567, each once within a row
- step_count: int32 [1], replicated, may hold values from 2 to 20
- embed_weight: float32 [1536, 768], P('row', 'col'), may hold values from -0.15625 to 0.15625
- embed_first: float32 [1536, 768], P('row', 'col'), may hold values from -9.1552734e-05 to 9.1552734e-05
- embed_second: float32 [1536, 768], P('row', 'col'), may hold values from 2.1121419e-11 to 3.379427e-10
- encoder_wide_weight: float32 [2, 768, 6144], P(None, 'row', 'col'), may hold values from -0.21875 to 0.21875
- encoder_wide_first: float32 [2, 768, 6144], P(None, 'row', 'col'), may hold values from -9.1552734e-05 to 9.1552734e-05
- encoder_wide_second: float32 [2, 768, 6144], P(None, 'row', 'col'), may hold values from 2.1121419e-11 to 3.379427e-10
- encoder_down_weight: float32 [2, 3072, 768], P(None, 'row', 'col'), may hold values from -0.109375 to 0.109375
- encoder_down_first: float32 [2, 3072, 768], P(None, 'row', 'col'), may hold values from -9.1552734e-05 to 9.1552734e-05
- encoder_down_second: float32 [2, 3072, 768], P(None, 'row', 'col'), may hold values from 2.1121419e-11 to 3.379427e-10
- decoder_wide_weight: float32 [384, 3072], P('row', 'col'), may hold values from -0.3125 to 0.3125
- decoder_wide_first: float32 [384, 3072], P('row', 'col'), may hold values from -9.1552734e-05 to 9.1552734e-05
- decoder_wide_second: float32 [384, 3072], P('row', 'col'), may hold values from 2.1121419e-11 to 3.379427e-10
- decoder_rows_weight: float32 [2304, 384], P('row', 'col'), may hold values from -0.15625 to 0.15625
- decoder_rows_first: float32 [2304, 384], P('row', 'col'), may hold values from -9.1552734e-05 to 9.1552734e-05
- decoder_rows_second: float32 [2304, 384], P('row', 'col'), may hold values from 2.1121419e-11 to 3.379427e-10
- pixel_head_weight: float32 [384, 1536], replicated, may hold values from -0.3125 to 0.3125
- pixel_head_first: float32 [384, 1536], replicated, may hold values from -9.1552734e-05 to 9.1552734e-05
- pixel_head_second: float32 [384, 1536], replicated, may hold values from 2.1121419e-11 to 3.379427e-10
- vectors_weight: float32 [5376], replicated, may hold values from 0.5 to 1.5
- vectors_first: float32 [5376], replicated, may hold values from -9.1552734e-05 to 9.1552734e-05
- vectors_second: float32 [5376], replicated, may hold values from 2.1121419e-11 to 3.379427e-10
Outputs:
- loss: float32 [], replicated
- new_embed_weight: float32 [1536, 768], P('row', 'col')
- new_embed_first: float32 [1536, 768], P('row', 'col')
- new_embed_second: float32 [1536, 768], P('row', 'col')
- new_encoder_wide_weight: float32 [2, 768, 6144], P(None, 'row', 'col')
- new_encoder_wide_first: float32 [2, 768, 6144], P(None, 'row', 'col')
- new_encoder_wide_second: float32 [2, 768, 6144], P(None, 'row', 'col')
- new_encoder_down_weight: float32 [2, 3072, 768], P(None, 'row', 'col')
- new_encoder_down_first: float32 [2, 3072, 768], P(None, 'row', 'col')
- new_encoder_down_second: float32 [2, 3072, 768], P(None, 'row', 'col')
- new_decoder_wide_weight: float32 [384, 3072], P('row', 'col')
- new_decoder_wide_first: float32 [384, 3072], P('row', 'col')
- new_decoder_wide_second: float32 [384, 3072], P('row', 'col')
- new_decoder_rows_weight: float32 [2304, 384], P('row', 'col')
- new_decoder_rows_first: float32 [2304, 384], P('row', 'col')
- new_decoder_rows_second: float32 [2304, 384], P('row', 'col')
- new_pixel_head_weight: float32 [384, 1536], replicated
- new_pixel_head_first: float32 [384, 1536], replicated
- new_pixel_head_second: float32 [384, 1536], replicated
- new_vectors_weight: float32 [5376], replicated
- new_vectors_first: float32 [5376], replicated
- new_vectors_second: float32 [5376], replicated
Inputs may be any that keep to these rules, and one draw needn't show every extreme that they name: Each row of tube_order is a permutation of the tube numbers of its clip; its first 157 entries are the visible tubes.
All inputs are finite; a program needn't handle non-finite values.
Results may differ from a plain program's by a relative error of at most 0.006.
The roundings to bfloat16 on the way count: a program that leaves them out, or rounds other values in their place, can miss the bound.
Values may be sent and summed in bfloat16 or wider, within the bound.
No kernel may reach another device: no remote copies, remote signals or barrier semaphores. Data moves between devices by JAX's collectives and lax.ppermute only.
A program may use at most 640 MiB of HBM per device.

v0:
```python
import jax
import jax.numpy as jnp
from jax import lax
from jax.sharding import PartitionSpec as P

D = 768
HEADS = 12
HDIM = 64
FF = 3072
DD = 384
DHEADS = 6
DFF = 1536
PIX = 1536
L = 2
NTUBE = 1568
NVIS = 157
NMASK = 1411


beta_first = 0.5
beta_second = 0.5
adam_epsilon = 1e-08
decay_factor = 0.05
norm_epsilon = 1e-06


def product(left, right):
    return jnp.dot(left, right, preferred_element_type=jnp.float32)


def product_left(left, right):
    return lax.dot_general(
        left, right, (((0,), (0,)), ((), ())), preferred_element_type=jnp.float32
    )


def product_right(left, right):
    return lax.dot_general(
        left, right, (((1,), (1,)), ((), ())), preferred_element_type=jnp.float32
    )


def sinusoid(count, width):
    places = jnp.arange(count, dtype=jnp.float32)[:, None]
    columns = jnp.arange(width // 2, dtype=jnp.float32)[None, :]
    angles = places * jnp.exp(columns * (-2.0 * jnp.log(10000.0) / width))
    return jnp.concatenate([jnp.sin(angles), jnp.cos(angles)], axis=1)


def layer_norm(values, gain):
    average = jnp.mean(values, axis=-1, keepdims=True)
    centred = values - average
    spread = jnp.mean(centred * centred, axis=-1, keepdims=True)
    return centred * lax.rsqrt(spread + norm_epsilon) * gain


def gelu_exact(values):
    return jax.nn.gelu(values, approximate=False)


def split_heads(packed, heads):
    length = packed.shape[0]
    width = packed.shape[1] // 3
    queries = packed[:, :width].reshape(length, heads, HDIM)
    keys = packed[:, width : 2 * width].reshape(length, heads, HDIM)
    values = packed[:, 2 * width :].reshape(length, heads, HDIM)
    blocks = 2 if length >= 1024 and length % 2 == 0 else 1
    return (queries, keys, values, blocks, length // blocks)


def attend(packed, heads):
    queries, keys, values, blocks, size = split_heads(packed, heads)
    scale = HDIM ** (-0.5)
    outputs = []
    totals = []
    for block in range(blocks):
        chosen = queries[block * size : (block + 1) * size]
        scores = (
            jnp.einsum("qhd,khd->hqk", chosen, keys, preferred_element_type=jnp.float32) * scale
        )
        largest = jnp.max(scores, axis=-1, keepdims=True)
        raised = jnp.exp(scores - largest)
        summed = jnp.sum(raised, axis=-1, keepdims=True)
        weights = (raised / summed).astype(jnp.bfloat16)
        outputs.append(
            jnp.einsum("hqk,khd->qhd", weights, values, preferred_element_type=jnp.float32)
        )
        totals.append(largest + jnp.log(summed))
    mixed = jnp.concatenate(outputs, axis=0)
    return (mixed.reshape(packed.shape[0], -1).astype(jnp.bfloat16), totals)


def attend_back(packed, totals, grad_mixed, heads):
    queries, keys, values, blocks, size = split_heads(packed, heads)
    length = packed.shape[0]
    scale = HDIM ** (-0.5)
    grad_out = grad_mixed.reshape(length, heads, HDIM)
    grad_keys = jnp.zeros(keys.shape, jnp.float32)
    grad_values = jnp.zeros(values.shape, jnp.float32)
    grad_queries = []
    for block in range(blocks):
        lower = block * size
        chosen = queries[lower : lower + size]
        chosen_grad = grad_out[lower : lower + size]
        scores = (
            jnp.einsum("qhd,khd->hqk", chosen, keys, preferred_element_type=jnp.float32) * scale
        )
        probs = jnp.exp(scores - totals[block])
        grad_probs = jnp.einsum(
            "qhd,khd->hqk", chosen_grad, values, preferred_element_type=jnp.float32
        )
        inner = jnp.sum(probs * grad_probs, axis=-1, keepdims=True)
        grad_scores = (probs * (grad_probs - inner)).astype(jnp.bfloat16)
        grad_queries.append(
            jnp.einsum("hqk,khd->qhd", grad_scores, keys, preferred_element_type=jnp.float32)
            * scale
        )
        grad_keys = (
            grad_keys
            + jnp.einsum("hqk,qhd->khd", grad_scores, chosen, preferred_element_type=jnp.float32)
            * scale
        )
        grad_values = grad_values + jnp.einsum(
            "hqk,qhd->khd",
            probs.astype(jnp.bfloat16),
            chosen_grad,
            preferred_element_type=jnp.float32,
        )
    combined = jnp.concatenate(
        [
            jnp.concatenate(grad_queries, axis=0).reshape(length, -1),
            grad_keys.reshape(length, -1),
            grad_values.reshape(length, -1),
        ],
        axis=1,
    )
    return combined.astype(jnp.bfloat16)


def layer_forward(stream, wide, down, gain_first, gain_second, heads):
    width = stream.shape[1]
    normed, back_first = jax.vjp(layer_norm, stream, gain_first)
    normed = normed.astype(jnp.bfloat16)
    packed = product(normed, wide[:, : 3 * width]).astype(jnp.bfloat16)
    mixed, totals = attend(packed, heads)
    middle = stream + product(mixed, wide[:, 3 * width : 4 * width])
    second, back_second = jax.vjp(layer_norm, middle, gain_second)
    second = second.astype(jnp.bfloat16)
    hidden = product(second, wide[:, 4 * width :])
    activated, back_gelu = jax.vjp(gelu_exact, hidden)
    activated = activated.astype(jnp.bfloat16)
    output = middle + product(activated, down)
    return (
        output,
        (back_first, normed, packed, mixed, totals, back_second, second, back_gelu, activated),
    )


def layer_backward(grad_stream, wide, down, kept, heads):
    back_first, normed, packed, mixed, totals, back_second, second, back_gelu, activated = kept
    width = grad_stream.shape[1]
    grad_branch = grad_stream.astype(jnp.bfloat16)
    grad_down = product_left(activated, grad_branch)
    grad_hidden = back_gelu(product_right(grad_branch, down))[0].astype(jnp.bfloat16)
    grad_up = product_left(second, grad_hidden)
    grad_middle, grad_gain_second = back_second(product_right(grad_hidden, wide[:, 4 * width :]))
    grad_middle = grad_stream + grad_middle
    grad_attend = grad_middle.astype(jnp.bfloat16)
    grad_output = product_left(mixed, grad_attend)
    grad_mixed = product_right(grad_attend, wide[:, 3 * width : 4 * width]).astype(jnp.bfloat16)
    grad_packed = attend_back(packed, totals, grad_mixed, heads)
    grad_qkv = product_left(normed, grad_packed)
    grad_before, grad_gain_first = back_first(product_right(grad_packed, wide[:, : 3 * width]))
    grad_wide = jnp.concatenate([grad_qkv, grad_output, grad_up], axis=1)
    return (grad_middle + grad_before, grad_wide, grad_down, grad_gain_first, grad_gain_second)


def clip_grads(weights, vectors, tube, order, inverse):
    embed, enc_wide, enc_down, dec_wide, dec_rows, head = weights
    visible = order[:NVIS]
    masked = order[NVIS:]
    base = (2 * L + 1) * D
    seen = jnp.take(tube, visible, axis=0)
    stream = product(seen, embed) + jnp.take(sinusoid(NTUBE, D), visible, axis=0)
    kept_layers = []
    for depth in range(L):
        stream, kept = layer_forward(
            stream,
            enc_wide[depth],
            enc_down[depth],
            vectors[2 * depth * D : (2 * depth + 1) * D],
            vectors[(2 * depth + 1) * D : (2 * depth + 2) * D],
            HEADS,
        )
        kept_layers.append(kept)
    normed, back_encoder = jax.vjp(layer_norm, stream, vectors[2 * L * D : base])
    normed = normed.astype(jnp.bfloat16)
    bridge = dec_rows[DFF:]
    bridged = product(normed, bridge)
    places = sinusoid(NTUBE, DD)
    token_mask = vectors[base + 3 * DD : base + 4 * DD]
    decoded = jnp.concatenate(
        [
            bridged + jnp.take(places, visible, axis=0),
            token_mask[None, :] + jnp.take(places, masked, axis=0),
        ],
        axis=0,
    )
    decoded, kept_decoder = layer_forward(
        decoded,
        dec_wide,
        dec_rows[:DFF],
        vectors[base : base + DD],
        vectors[base + DD : base + 2 * DD],
        DHEADS,
    )
    final, back_final = jax.vjp(layer_norm, decoded[NVIS:], vectors[base + 2 * DD : base + 3 * DD])
    final = final.astype(jnp.bfloat16)
    predicted = product(final, head)
    target = layer_norm(jnp.take(tube, masked, axis=0).astype(jnp.float32), 1.0)
    error = predicted - target
    loss_value = jnp.sum(error * error) * inverse
    grad_predicted = (2.0 * inverse * error).astype(jnp.bfloat16)
    grad_head = product_left(final, grad_predicted)
    grad_tail, grad_gain_final = back_final(product_right(grad_predicted, head))
    grad_decoded = jnp.concatenate([jnp.zeros((NVIS, DD), jnp.float32), grad_tail], axis=0)
    grad_decoded, grad_dec_wide, grad_dec_down, dec_gain_first, dec_gain_second = layer_backward(
        grad_decoded, dec_wide, dec_rows[:DFF], kept_decoder, DHEADS
    )
    grad_token = jnp.sum(grad_decoded[NVIS:], axis=0)
    grad_bridged = grad_decoded[:NVIS].astype(jnp.bfloat16)
    grad_bridge = product_left(normed, grad_bridged)
    grad_stream, grad_gain_encoder = back_encoder(product_right(grad_bridged, bridge))
    wide_grads = [None] * L
    down_grads = [None] * L
    gain_grads = [None] * L
    for depth in reversed(range(L)):
        grad_stream, wide_grads[depth], down_grads[depth], first_gain, second_gain = layer_backward(
            grad_stream, enc_wide[depth], enc_down[depth], kept_layers[depth], HEADS
        )
        gain_grads[depth] = jnp.concatenate([first_gain, second_gain])
    grad_embed = product_left(seen, grad_stream.astype(jnp.bfloat16))
    grad_vectors = jnp.concatenate(
        gain_grads
        + [grad_gain_encoder, dec_gain_first, dec_gain_second, grad_gain_final, grad_token]
    )
    grads = (
        grad_embed,
        jnp.stack(wide_grads),
        jnp.stack(down_grads),
        grad_dec_wide,
        jnp.concatenate([grad_dec_down, grad_bridge], axis=0),
        grad_head,
        grad_vectors,
    )
    return (loss_value, grads)


def adam_update(master, moment, second, grad, rate, decay, count):
    moment = beta_first * moment + (1.0 - beta_first) * grad
    second = beta_second * second + (1.0 - beta_second) * grad * grad
    first_hat = moment / (1.0 - beta_first**count)
    second_hat = second / (1.0 - beta_second**count)
    master = master - rate * (first_hat / (jnp.sqrt(second_hat) + adam_epsilon) + decay * master)
    return (master, moment, second)


def shards(
    tubes,
    tube_order,
    step_count,
    embed_weight,
    embed_first,
    embed_second,
    encoder_wide_weight,
    encoder_wide_first,
    encoder_wide_second,
    encoder_down_weight,
    encoder_down_first,
    encoder_down_second,
    decoder_wide_weight,
    decoder_wide_first,
    decoder_wide_second,
    decoder_rows_weight,
    decoder_rows_first,
    decoder_rows_second,
    pixel_head_weight,
    pixel_head_first,
    pixel_head_second,
    vectors_weight,
    vectors_first,
    vectors_second,
):
    low_embed = embed_weight.astype(jnp.bfloat16)
    low_enc_wide = encoder_wide_weight.astype(jnp.bfloat16)
    low_enc_down = encoder_down_weight.astype(jnp.bfloat16)
    low_dec_wide = decoder_wide_weight.astype(jnp.bfloat16)
    low_dec_rows = decoder_rows_weight.astype(jnp.bfloat16)
    across = (
        lax.all_gather(low_embed, "col", axis=1, tiled=True),
        lax.all_gather(low_enc_wide, "col", axis=2, tiled=True),
        lax.all_gather(low_enc_down, "col", axis=2, tiled=True),
        lax.all_gather(low_dec_wide, "col", axis=1, tiled=True),
        lax.all_gather(low_dec_rows, "col", axis=1, tiled=True),
    )
    whole = (
        lax.all_gather(across[0], "row", axis=0, tiled=True),
        lax.all_gather(across[1], "row", axis=1, tiled=True),
        lax.all_gather(across[2], "row", axis=1, tiled=True),
        lax.all_gather(across[3], "row", axis=0, tiled=True),
        lax.all_gather(across[4], "row", axis=0, tiled=True),
    )
    weights = tuple(whole) + (pixel_head_weight.astype(jnp.bfloat16),)
    inverse = 1.0 / (tubes.shape[0] * lax.axis_size("row") * lax.axis_size("col") * NMASK * PIX)
    loss_local = jnp.zeros((), jnp.float32)
    totals = None
    for clip in range(tubes.shape[0]):
        value, grads = clip_grads(weights, vectors_weight, tubes[clip], tube_order[clip], inverse)
        loss_local = loss_local + value
        totals = grads if totals is None else jax.tree.map(jnp.add, totals, grads)
    partial_value = (
        lax.psum_scatter(
            totals[0].astype(jnp.bfloat16), "row", scatter_dimension=0, tiled=True
        ).astype(jnp.float32),
        lax.psum_scatter(
            totals[1].astype(jnp.bfloat16), "row", scatter_dimension=1, tiled=True
        ).astype(jnp.float32),
        lax.psum_scatter(
            totals[2].astype(jnp.bfloat16), "row", scatter_dimension=1, tiled=True
        ).astype(jnp.float32),
        lax.psum_scatter(
            totals[3].astype(jnp.bfloat16), "row", scatter_dimension=0, tiled=True
        ).astype(jnp.float32),
        lax.psum_scatter(
            totals[4].astype(jnp.bfloat16), "row", scatter_dimension=0, tiled=True
        ).astype(jnp.float32),
    )
    owned = (
        lax.psum_scatter(partial_value[0], "col", scatter_dimension=1, tiled=True),
        lax.psum_scatter(partial_value[1], "col", scatter_dimension=2, tiled=True),
        lax.psum_scatter(partial_value[2], "col", scatter_dimension=2, tiled=True),
        lax.psum_scatter(partial_value[3], "col", scatter_dimension=1, tiled=True),
        lax.psum_scatter(partial_value[4], "col", scatter_dimension=1, tiled=True),
    )
    loss, grad_head, grad_vectors = lax.psum((loss_local, totals[5], totals[6]), ("row", "col"))
    grads = tuple(owned) + (grad_head, grad_vectors)
    masters = (
        embed_weight,
        encoder_wide_weight,
        encoder_down_weight,
        decoder_wide_weight,
        decoder_rows_weight,
        pixel_head_weight,
        vectors_weight,
    )
    firsts = (
        embed_first,
        encoder_wide_first,
        encoder_down_first,
        decoder_wide_first,
        decoder_rows_first,
        pixel_head_first,
        vectors_first,
    )
    seconds = (
        embed_second,
        encoder_wide_second,
        encoder_down_second,
        decoder_wide_second,
        decoder_rows_second,
        pixel_head_second,
        vectors_second,
    )
    count = step_count[0].astype(jnp.float32)
    rates = (
        PIX ** (-0.5),
        D ** (-0.5),
        FF ** (-0.5),
        DD ** (-0.5),
        DFF ** (-0.5),
        DD ** (-0.5),
        0.1,
    )
    decays = (decay_factor,) * 6 + (0.0,)
    results = [loss]
    for index in range(7):
        results.extend(
            adam_update(
                masters[index],
                firsts[index],
                seconds[index],
                grads[index],
                rates[index],
                decays[index],
                count,
            )
        )
    return tuple(results)


def solution(mesh):
    placed = (
        P(("row", "col"), None, None),
        P(("row", "col"), None),
        P(),
        P("row", "col"),
        P("row", "col"),
        P("row", "col"),
        P(None, "row", "col"),
        P(None, "row", "col"),
        P(None, "row", "col"),
        P(None, "row", "col"),
        P(None, "row", "col"),
        P(None, "row", "col"),
        P("row", "col"),
        P("row", "col"),
        P("row", "col"),
        P("row", "col"),
        P("row", "col"),
        P("row", "col"),
        P(),
        P(),
        P(),
        P(),
        P(),
        P(),
    )
    return jax.shard_map(
        shards,
        mesh=mesh,
        in_specs=placed,
        out_specs=(
            P(),
            P("row", "col"),
            P("row", "col"),
            P("row", "col"),
            P(None, "row", "col"),
            P(None, "row", "col"),
            P(None, "row", "col"),
            P(None, "row", "col"),
            P(None, "row", "col"),
            P(None, "row", "col"),
            P("row", "col"),
            P("row", "col"),
            P("row", "col"),
            P("row", "col"),
            P("row", "col"),
            P("row", "col"),
            P(),
            P(),
            P(),
            P(),
            P(),
            P(),
        ),
        check_vma=False,
    )
```

profile of v0, /device:TPU:0, one launch (start us, length us, event | category | flops | bytes accessed | tf_op | source)
XLA Modules:
  0.0 2145.3 jit_solution(14863647534181687388)
XLA Ops:
  29.3 35.9 %all-gather.10.cloned.1.call-done = bf16[2,192,6144]{2,1,0:T(8,128)(2,1)} async-done(((bf16[2,192,768]{2,1,0:T(8,128)(2,1)}), bf16[2,192,6144]{2,1,0:T(8,128)(2,1)}) %all-gather.10.cloned.1.call-update) | async-done | bytes 4718608 | tf_op jit(solution)/shard_map/all_gather | solution.py:301
  65.3 32.4 %all-gather.14.cloned.1.call-done = bf16[2,768,768]{1,2,0:T(8,128)(2,1)} async-done(((bf16[2,768,96]{1,2,0:T(8,128)(2,1)}), bf16[2,768,768]{1,2,0:T(8,128)(2,1)}) %all-gather.14.cloned.1.call-update) | async-done | bytes 2359312 | tf_op jit(solution)/shard_map/all_gather | solution.py:302
  237.0 75.6 %all-gather.12.cloned.1.call-done = bf16[2,768,6144]{2,1,0:T(8,128)(2,1)} async-done(((bf16[2,192,6144]{2,1,0:T(8,128)(2,1)}), bf16[2,768,6144]{2,1,0:T(8,128)(2,1)}) %all-gather.12.cloned.1.call-update) | async-done | bytes 18874384 | tf_op jit(solution)/shard_map/all_gather | solution.py:308
  349.1 61.4 %all-gather.16.cloned.1.call-done = bf16[2,3072,768]{1,2,0:T(8,128)(2,1)} async-done(((bf16[2,768,768]{1,2,0:T(8,128)(2,1)}), bf16[2,3072,768]{1,2,0:T(8,128)(2,1)}) %all-gather.16.cloned.1.call-update) | async-done | bytes 9437200 | tf_op jit(solution)/shard_map/all_gather | solution.py:309
  451.2 33.4 %all-gather.20.cloned.1.call-done = bf16[384,3072]{1,0:T(8,128)(2,1)} async-done(((bf16[96,3072]{1,0:T(8,128)(2,1)}), bf16[384,3072]{1,0:T(8,128)(2,1)}) %all-gather.20.cloned.1.call-update) | async-done | bytes 2359312 | tf_op jit(solution)/shard_map/all_gather | solution.py:310
  729.6 25.0 %multiply_convert_fusion.4 = (bf16[1568,1536]{1,0:T(8,128)(2,1)S(1)}, f32[1568,1536]{1,0:T(8,128)}, f32[1568,1536]{1,0:T(8,128)}) fusion(bf16[384,3072]{1,0:T(8,128)(2,1)S(1)} %copy-done.243, f32[1568,384]{1,0:T(8,128)S(1)} %get-tuple-element.343, f32[1568]{0:T(1024)S(1)} %fusion.257, f32[1568]{0:T(1024)S(1)} %broadcast_multiply_fusion.4, ...), kind=kOutput, calls=%fused_computation.72 | convolution fusion | flops 2008645632 | bytes 27691008 | tf_op jit(solution)/shard_map/dot_general | solution.py:28
  763.3 24.9 %multiply_convert_fusion.5 = (bf16[1568,1536]{1,0:T(8,128)(2,1)S(1)}, f32[1568,1536]{1,0:T(8,128)}, f32[1568,1536]{1,0:T(8,128)}) fusion(bf16[384,3072]{1,0:T(8,128)(2,1)S(1)} %copy-done.243, f32[1568,384]{1,0:T(8,128)S(1)} %get-tuple-element.318, f32[384]{0:T(512)S(1)} %copy-done.420, f32[1568]{0:T(1024)S(1)} %fusion.254, ...), kind=kOutput, calls=%fused_computation.85 | convolution fusion | flops 2008645632 | bytes 27691008 | tf_op jit(solution)/shard_map/dot_general | solution.py:28
  863.6 24.4 %multiply_reduce_fusion.3 = (f32[6,784]{1,0:T(8,128)S(1)}, f32[6,784,1568]{2,1,0:T(8,128)}) fusion(f32[6,784,1568]{2,1,0:T(8,128)} %get-tuple-element.316, f32[6,784]{1,0:T(8,128)S(1)} %copy-done.157, bf16[784,6,64]{0,2,1:T(8,128)(2,1)} %bitcast.338, bf16[1568,6,64]{0,2,1:T(8,128)(2,1)S(1)} %bitcast.332), kind=kOutput, calls=%fused_computation.22 | convolution fusion | flops 973610368 | bytes 60850944 | tf_op jit(solution)/shard_map/qhd,khd->hqk/dot_general | solution.py:109
  888.0 25.7 %multiply_convert_fusion.3 = bf16[6,784,1568]{2,1,0:T(8,128)(2,1)} fusion(f32[6,784,1568]{2,1,0:T(8,128)} %get-tuple-element.354, f32[6,784,1568]{2,1,0:T(8,128)} %get-tuple-element.316, f32[6,784]{1,0:T(8,128)S(1)} %get-tuple-element.353, f32[6,784]{1,0:T(8,128)S(1)} %copy-done.157), kind=kLoop, calls=%fused_computation.21 | loop fusion | flops 36879360 | bytes 73796352 | tf_op jit(solution)/shard_map/convert_element_type | solution.py:113
  950.2 24.9 %multiply_reduce_fusion.2 = (f32[6,784]{1,0:T(8,128)S(1)}, f32[6,784,1568]{2,1,0:T(8,128)}) fusion(f32[6,784,1568]{2,1,0:T(8,128)} %get-tuple-element.314, f32[6,784]{1,0:T(8,128)S(1)} %copy-done.155, bf16[784,6,64]{0,2,1:T(8,128)(2,1)S(1)} %bitcast.343, bf16[1568,6,64]{0,2,1:T(8,128)(2,1)S(1)} %bitcast.333), kind=kOutput, calls=%fused_computation.19 | convolution fusion | flops 973610368 | bytes 60850944 | tf_op jit(solution)/shard_map/qhd,khd->hqk/dot_general | solution.py:109
  978.6 24.1 %multiply_reduce_fusion.1 = (f32[6,784]{1,0:T(8,128)S(1)}, f32[6,784,1568]{2,1,0:T(8,128)}) fusion(f32[6,784,1568]{2,1,0:T(8,128)} %get-tuple-element.341, f32[6,784]{1,0:T(8,128)S(1)} %copy-done.156, bf16[784,6,64]{0,2,1:T(8,128)(2,1)S(1)} %bitcast.340, bf16[1568,6,64]{0,2,1:T(8,128)(2,1)S(1)} %bitcast.328), kind=kOutput, calls=%fused_computation.16 | convolution fusion | flops 973610368 | bytes 60850944 | tf_op jit(solution)/shard_map/qhd,khd->hqk/dot_general | solution.py:109
  1002.7 25.6 %multiply_convert_fusion.1 = bf16[6,784,1568]{2,1,0:T(8,128)(2,1)} fusion(f32[6,784,1568]{2,1,0:T(8,128)} %get-tuple-element.350, f32[6,784,1568]{2,1,0:T(8,128)} %get-tuple-element.341, f32[6,784]{1,0:T(8,128)S(1)} %get-tuple-element.349, f32[6,784]{1,0:T(8,128)S(1)} %copy-done.156), kind=kLoop, calls=%fused_computation.15 | loop fusion | flops 36879360 | bytes 73796352 | tf_op jit(solution)/shard_map/convert_element_type | solution.py:113
  1064.3 24.1 %multiply_reduce_fusion = (f32[6,784]{1,0:T(8,128)S(1)}, f32[6,784,1568]{2,1,0:T(8,128)}) fusion(f32[6,784,1568]{2,1,0:T(8,128)} %get-tuple-element.339, f32[6,784]{1,0:T(8,128)S(1)} %copy-done.154, bf16[784,6,64]{0,2,1:T(8,128)(2,1)S(1)} %bitcast.345, bf16[1568,6,64]{0,2,1:T(8,128)(2,1)S(1)} %bitcast.329), kind=kOutput, calls=%fused_computation.13 | convolution fusion | flops 973610368 | bytes 60850944 | tf_op jit(solution)/shard_map/qhd,khd->hqk/dot_general | solution.py:109
  1116.2 25.6 %multiply_convert_fusion.2 = bf16[6,784,1568]{2,1,0:T(8,128)(2,1)} fusion(f32[6,784,1568]{2,1,0:T(8,128)} %get-tuple-element.356, f32[6,784,1568]{2,1,0:T(8,128)} %get-tuple-element.314, f32[6,784]{1,0:T(8,128)S(1)} %get-tuple-element.355, f32[6,784]{1,0:T(8,128)S(1)} %copy-done.155), kind=kLoop, calls=%fused_computation.18 | loop fusion | flops 36879360 | bytes 73796352 | tf_op jit(solution)/shard_map/convert_element_type | solution.py:113
  1162.7 25.9 %multiply_convert_fusion = bf16[6,784,1568]{2,1,0:T(8,128)(2,1)} fusion(f32[6,784,1568]{2,1,0:T(8,128)} %get-tuple-element.352, f32[6,784,1568]{2,1,0:T(8,128)} %get-tuple-element.339, f32[6,784]{1,0:T(8,128)S(1)} %get-tuple-element.351, f32[6,784]{1,0:T(8,128)S(1)} %copy-done.154), kind=kLoop, calls=%fused_computation.12 | loop fusion | flops 36879360 | bytes 73796352 | tf_op jit(solution)/shard_map/convert_element_type | solution.py:113
  1441.2 32.8 %fusion = bf16[2,768,6144]{2,1,0:T(8,128)(2,1)} fusion(f32[1,768,6144]{2,1,0:T(8,128)} %maximum_bitcast_fusion.1, f32[1,768,6144]{2,1,0:T(8,128)} %maximum_bitcast_fusion, f32[1,768,6144]{2,1,0:T(8,128)} %maximum_bitcast_fusion.3, f32[1,768,6144]{2,1,0:T(8,128)} %maximum_bitcast_fusion.2), kind=kLoop, calls=%fused_computation.11 | loop fusion | flops 37748736 | bytes 94371840 | tf_op jit(solution)/shard_map/convert_element_type | solution.py:326
  1515.3 166.4 %reduce-scatter.16.cloned.1.call-done = bf16[2,192,6144]{2,1,0:T(8,128)(2,1)} async-done(((bf16[2,768,6144]{2,1,0:T(8,128)(2,1)}), bf16[2,192,6144]{2,1,0:T(8,128)(2,1)}) %reduce-scatter.16.cloned.1.call-update) | async-done | bytes 4718608 | tf_op jit(solution)/shard_map/reduce_scatter | solution.py:325
  1695.3 40.1 %all-reduce.3 = (f32[]{:T(128)}, f32[5376]{0:T(1024)S(1)}) all-reduce(f32[]{:T(128)S(6)} %multiply.408, f32[5376]{0:T(1024)S(1)} %add.655), channel_id=1, replica_groups=mesh['row'=4,'col'=8] {'row','col'}, use_global_device_ids=true, to_apply=%region_54.60 | all-reduce | flops 5377 | bytes 43016 | tf_op jit(solution)/shard_map/psum | solution.py:345
  1736.1 87.6 %all-reduce.7.cloned.1.call-done = f32[384,1536]{1,0:T(8,128)} async-done(((f32[384,1536]{1,0:T(8,128)}), f32[384,1536]{1,0:T(8,128)}) %all-reduce.7.cloned.1.call-update) | async-done | bytes 2359312 | tf_op jit(solution)/shard_map/psum | solution.py:345
  1831.6 26.2 %reduce-scatter.30.cloned.1.call-done = f32[48,576]{1,0:T(8,128)} async-done(((f32[384,576]{1,0:T(8,128)}), f32[48,576]{1,0:T(8,128)}) %reduce-scatter.30.cloned.1.call-update) | async-done | bytes 110608
  1859.5 32.4 %reduce-scatter.24.cloned.1.call-done = f32[96,384]{1,0:T(8,128)} async-done(((f32[96,3072]{1,0:T(8,128)}), f32[96,384]{1,0:T(8,128)}) %reduce-scatter.24.cloned.1.call-update) | async-done | bytes 147472 | tf_op jit(solution)/shard_map/reduce_scatter | solution.py:342
  1893.6 32.0 %reduce-scatter.28.cloned.1.call-done = f32[96,384]{1,0:T(8,128)} async-done(((f32[768,384]{1,0:T(8,128)}), f32[96,384]{1,0:T(8,128)}) %reduce-scatter.28.cloned.1.call-update) | async-done | bytes 147472
  1927.4 105.1 %all-reduce.9.cloned.1.call-done = f32[2,768,768]{1,0,2:T(2,128)} async-done(((f32[2,768,768]{1,0,2:T(2,128)}), f32[2,768,768]{1,0,2:T(2,128)}) %all-reduce.9.cloned.1.call-update) | async-done | bytes 4718608
  2036.4 97.8 %reduce-scatter.18.cloned.1.call-done = f32[2,192,768]{2,1,0:T(8,128)} async-done(((f32[2,192,6144]{2,1,0:T(8,128)}), f32[2,192,768]{2,1,0:T(8,128)}) %reduce-scatter.18.cloned.1.call-update) | async-done | bytes 1179664 | tf_op jit(solution)/shard_map/reduce_scatter | solution.py:340
  (1423 shorter events, 1012.3 us)
Async XLA Ops:
  7.2 58.0 %all-gather.10.cloned.1.call-start = ((), (), s32[]{:S(2)}) async-start(), calls=%async_computation.10 | async-start | bytes 5308416 | tf_op jit(solution)/shard_map/all_gather | solution.py:301
  9.5 88.2 %all-gather.14.cloned.1.call-start = ((), (), s32[]{:S(2)}) async-start(), calls=%async_computation.12 | async-start | bytes 2654208 | tf_op jit(solution)/shard_map/all_gather | solution.py:302
  10.3 220.9 %all-gather.8.cloned.1.call-start = ((), (), s32[]{:S(2)}) async-start(), calls=%async_computation.9 | async-start | bytes 2949120 | tf_op jit(solution)/shard_map/all_gather | solution.py:307
  29.3 283.3 %all-gather.12.cloned.1.call-start = ((), (), s32[]{:S(2)}) async-start(), calls=%async_computation.11 | async-start | bytes 23592960 | tf_op jit(solution)/shard_map/all_gather | solution.py:308
  65.3 345.3 %all-gather.16.cloned.1.call-start = ((), (), s32[]{:S(2)}) async-start(), calls=%async_computation.13 | async-start | bytes 11796480 | tf_op jit(solution)/shard_map/all_gather | solution.py:309
  97.7 347.6 %all-gather.18.cloned.1.call-start = ((), (), s32[]{:S(2)}) async-start(), calls=%async_computation.14 | async-start | bytes 2211840 | tf_op jit(solution)/shard_map/all_gather | solution.py:311
  113.4 371.1 %all-gather.20.cloned.1.call-start = ((), (), s32[]{:S(2)}) async-start(), calls=%async_computation.15 | async-start | bytes 2949120 | tf_op jit(solution)/shard_map/all_gather | solution.py:310
  129.6 1359.4 %reduce-scatter.26.cloned.1.call-start = ((), (), s32[]{:S(2)}) async-start(), calls=%async_computation.22 | async-start | bytes 2211840 | tf_op jit(solution)/shard_map/reduce_scatter | solution.py:334
  131.3 193.2 %copy-start.256 = (f32[768]{0:T(1024)}, f32[768]{0:T(1024)S(1)}, u32[]{:S(2)}) copy-start(f32[768]{0:T(1024)S(1)} %get-tuple-element.256) | copy-start | bytes 9220
  131.3 395.1 %copy-start.248 = (f32[768]{0:T(1024)}, f32[768]{0:T(1024)S(1)}, u32[]{:S(2)}) copy-start(f32[768]{0:T(1024)S(1)} %get-tuple-element.253) | copy-start | bytes 9220
  231.2 308.7 %copy-start.3 = (f32[1411,384]{1,0:T(8,128)}, f32[1411,384]{1,0:T(8,128)S(1)}, u32[]{:S(2)}) copy-start(f32[1411,384]{1,0:T(8,128)S(1)} %get-tuple-element.291) | copy-start | bytes 6501892
  234.8 266.2 %copy-start.48 = (f32[157,768]{1,0:T(8,128)}, f32[157,768]{1,0:T(8,128)S(1)}, u32[]{:S(2)}) copy-start(f32[157,768]{1,0:T(8,128)S(1)} %get-tuple-element.323) | copy-start | bytes 1446916
  1295.9 195.4 %reduce-scatter.22.cloned.1.call-start = ((), (), s32[]{:S(2)}) async-start(), calls=%async_computation.20 | async-start | bytes 2949120 | tf_op jit(solution)/shard_map/reduce_scatter | solution.py:331
  1322.6 171.0 %reduce-scatter.14.cloned.1.call-start = ((), (), s32[]{:S(2)}) async-start(), calls=%async_computation.16 | async-start | bytes 2949120 | tf_op jit(solution)/shard_map/reduce_scatter | solution.py:322
  1341.5 166.5 %reduce-scatter.20.cloned.1.call-start = ((), (), s32[]{:S(2)}) async-start(), calls=%async_computation.19 | async-start | bytes 11796480 | tf_op jit(solution)/shard_map/reduce_scatter | solution.py:328
  1362.4 319.3 %reduce-scatter.16.cloned.1.call-start = ((), (), s32[]{:S(2)}) async-start(), calls=%async_computation.17 | async-start | bytes 23592960 | tf_op jit(solution)/shard_map/reduce_scatter | solution.py:325
  1474.2 349.5 %all-reduce.7.cloned.1.call-start = ((), (), s32[]{:S(2)}) async-start(), calls=%async_computation.23 | async-start | bytes 4718592 | tf_op jit(solution)/shard_map/psum | solution.py:345
  1489.0 368.9 %reduce-scatter.30.cloned.1.call-start = ((), (), s32[]{:S(2)}) async-start(), calls=%async_computation.25 | async-start | bytes 1105920
  1491.3 400.6 %reduce-scatter.24.cloned.1.call-start = ((), (), s32[]{:S(2)}) async-start(), calls=%async_computation.21 | async-start | bytes 1327104 | tf_op jit(solution)/shard_map/reduce_scatter | solution.py:342
  1493.6 432.1 %reduce-scatter.28.cloned.1.call-start = ((), (), s32[]{:S(2)}) async-start(), calls=%async_computation.24 | async-start | bytes 1327104
  1496.0 536.5 %all-reduce.9.cloned.1.call-start = ((), (), s32[]{:S(2)}) async-start(), calls=%async_computation.26 | async-start | bytes 9437184
  1515.2 619.0 %reduce-scatter.18.cloned.1.call-start = ((), (), s32[]{:S(2)}) async-start(), calls=%async_computation.18 | async-start | bytes 10616832 | tf_op jit(solution)/shard_map/reduce_scatter | solution.py:340
  1831.6 202.0 %copy-start.164 = (f32[2,768,96]{1,2,0:T(8,128)S(1)}, f32[2,768,96]{1,2,0:T(8,128)}, u32[]{:S(2)}) copy-start(f32[2,768,96]{1,2,0:T(8,128)} %param.43) | copy-start | bytes 1769476
  1831.6 202.0 %copy-start.238 = (f32[2,768,96]{1,2,0:T(8,128)S(1)}, f32[2,768,96]{1,2,0:T(8,128)}, u32[]{:S(2)}) copy-start(f32[2,768,96]{1,2,0:T(8,128)} %param.45) | copy-start | bytes 1769476
  (483 other events, 5900.6 us)
Sparse Core Ops, SparseCore 0:
  10.2 54.9 all-gather.9
  67.4 30.2 all-gather.13
  99.5 36.4 all-gather.7
  137.7 174.8 all-gather.11
  314.3 96.1 all-gather.15
  412.8 32.4 all-gather.17
  447.1 37.3 all-gather.19
  1296.0 32.4 reduce-scatter.25
  1331.6 37.3 reduce-scatter.21
  1372.5 37.3 reduce-scatter.13
  1413.0 94.8 reduce-scatter.19
  1510.9 170.7 reduce-scatter.15
  1687.8 135.8 all-reduce.6
  1826.4 31.4 reduce-scatter.29
  1860.5 31.3 reduce-scatter.23
  1894.6 31.0 reduce-scatter.27
  1927.9 104.5 all-reduce.8
  2034.7 99.4 reduce-scatter.17
where the time goes:
time: 2150 us
  waiting for transfers between devices  804 us (37%)
  matrix products  688 us (32%)
  other arithmetic  349 us (16%)
  local copies, waits for them, and re-layouts  189 us (9%)
  blocking collectives  89.6 us (4%)
  between operations  23.9 us (1%)
    reduce_scatter x1, waiting for transfers between devices, shards(): lax.psum_scatter(totals[1].astype(jnp.bfloat16), 'row', scatter_dimension...  166 us
    unnamed x21, waiting for transfers between devices  164 us
    dot_general x30, matrix products, product(): return jnp.dot(left, right, preferred_element_type=jnp.float32)  141 us
    convert_element_type x8, other arithmetic, attend_back(): grad_scores = (probs * (grad_probs - inner)).astype(jnp.bfloat16)  105 us
    dot_general x8, matrix products, attend_back(): jnp.einsum('qhd,khd->hqk', chosen_grad, values, preferred_element_type=jn...  102 us
    reduce_scatter x1, waiting for transfers between devices, shards(): lax.psum_scatter(partial_value[1], 'col', scatter_dimension=2, tiled=True)  97.8 us
    dot_general x28, matrix products, product_right(): lax.dot_general(left, right, (((1,), (1,)), ((), ())), preferred_element_...  94.5 us
    psum x1, waiting for transfers between devices, shards(): lax.psum((loss_local, totals[5], totals[6]), ('row', 'col'))  87.6 us
  transfers between devices with their start and end apart: 18, of which 14 were waited for; matrix products, arithmetic and copies ran while one was open for 18% of the time, Pallas kernels for 0%

commit v1 on v0

--- a/solution.py
+++ b/solution.py
@@ -149,7 +149,7 @@
     hidden = product(second, wide[:, 4 * width :])
     activated, back_gelu = jax.vjp(gelu_exact, hidden)
     activated = activated.astype(jnp.bfloat16)
-    output = middle + product(activated, down)
+    output = middle + product_right(activated, down)
     return (
         output,
         (back_first, normed, packed, mixed, totals, back_second, second, back_gelu, activated),
@@ -160,8 +160,8 @@
     back_first, normed, packed, mixed, totals, back_second, second, back_gelu, activated = kept
     width = grad_stream.shape[1]
     grad_branch = grad_stream.astype(jnp.bfloat16)
-    grad_down = product_left(activated, grad_branch)
-    grad_hidden = back_gelu(product_right(grad_branch, down))[0].astype(jnp.bfloat16)
+    grad_down = product_left(grad_branch, activated)
+    grad_hidden = back_gelu(product(grad_branch, down))[0].astype(jnp.bfloat16)
     grad_up = product_left(second, grad_hidden)
     grad_middle, grad_gain_second = back_second(product_right(grad_hidden, wide[:, 4 * width :]))
     grad_middle = grad_stream + grad_middle
@@ -181,7 +181,7 @@
     masked = order[NVIS:]
     base = (2 * L + 1) * D
     seen = jnp.take(tube, visible, axis=0)
-    stream = product(seen, embed) + jnp.take(sinusoid(NTUBE, D), visible, axis=0)
+    stream = product_right(seen, embed) + jnp.take(sinusoid(NTUBE, D), visible, axis=0)
     kept_layers = []
     for depth in range(L):
         stream, kept = layer_forward(
@@ -195,8 +195,8 @@
         kept_layers.append(kept)
     normed, back_encoder = jax.vjp(layer_norm, stream, vectors[2 * L * D : base])
     normed = normed.astype(jnp.bfloat16)
-    bridge = dec_rows[DFF:]
-    bridged = product(normed, bridge)
+    bridge = dec_rows[:, DFF:]
+    bridged = product_right(normed, bridge)
     places = sinusoid(NTUBE, DD)
     token_mask = vectors[base + 3 * DD : base + 4 * DD]
     decoded = jnp.concatenate(
@@ -209,7 +209,7 @@
     decoded, kept_decoder = layer_forward(
         decoded,
         dec_wide,
-        dec_rows[:DFF],
+        dec_rows[:, :DFF],
         vectors[base : base + DD],
         vectors[base + DD : base + 2 * DD],
         DHEADS,
@@ -225,12 +225,12 @@
     grad_tail, grad_gain_final = back_final(product_right(grad_predicted, head))
     grad_decoded = jnp.concatenate([jnp.zeros((NVIS, DD), jnp.float32), grad_tail], axis=0)
     grad_decoded, grad_dec_wide, grad_dec_down, dec_gain_first, dec_gain_second = layer_backward(
-        grad_decoded, dec_wide, dec_rows[:DFF], kept_decoder, DHEADS
+        grad_decoded, dec_wide, dec_rows[:, :DFF], kept_decoder, DHEADS
     )
     grad_token = jnp.sum(grad_decoded[NVIS:], axis=0)
     grad_bridged = grad_decoded[:NVIS].astype(jnp.bfloat16)
-    grad_bridge = product_left(normed, grad_bridged)
-    grad_stream, grad_gain_encoder = back_encoder(product_right(grad_bridged, bridge))
+    grad_bridge = product_left(grad_bridged, normed)
+    grad_stream, grad_gain_encoder = back_encoder(product(grad_bridged, bridge))
     wide_grads = [None] * L
     down_grads = [None] * L
     gain_grads = [None] * L
@@ -239,21 +239,92 @@
             grad_stream, enc_wide[depth], enc_down[depth], kept_layers[depth], HEADS
         )
         gain_grads[depth] = jnp.concatenate([first_gain, second_gain])
-    grad_embed = product_left(seen, grad_stream.astype(jnp.bfloat16))
+    grad_embed = product_left(grad_stream.astype(jnp.bfloat16), seen)
     grad_vectors = jnp.concatenate(
         gain_grads
         + [grad_gain_encoder, dec_gain_first, dec_gain_second, grad_gain_final, grad_token]
     )
     grads = (
         grad_embed,
-        jnp.stack(wide_grads),
-        jnp.stack(down_grads),
+        tuple(wide_grads),
+        tuple(down_grads),
         grad_dec_wide,
-        jnp.concatenate([grad_dec_down, grad_bridge], axis=0),
+        jnp.concatenate([grad_dec_down, grad_bridge], axis=1),
         grad_head,
         grad_vectors,
     )
     return (loss_value, grads)
+
+
+def pack_block(block, width):
+    height, breadth = block.shape[-2:]
+    lead = block.shape[:-2]
+    if breadth == width:
+        return block
+    if width % breadth == 0 and height % (width // breadth) == 0:
+        times = width // breadth
+        split = block.reshape(lead + (times, height // times, breadth))
+        return jnp.concatenate([split[..., part, :, :] for part in range(times)], axis=-1)
+    return block.reshape(lead + (height * breadth // width, width))
+
+
+def unpack_block(block, height, breadth):
+    width = block.shape[-1]
+    lead = block.shape[:-2]
+    if breadth == width:
+        return block
+    if width % breadth == 0 and height % (width // breadth) == 0:
+        times = width // breadth
+        return jnp.concatenate(
+            [block[..., part * breadth : (part + 1) * breadth] for part in range(times)], axis=-2
+        )
+    return block.reshape(lead + (height, breadth))
+
+
+def group_width(shapes):
+    return next(iter(shapes))[1]
+
+
+def gather_group(pieces, rows, cols):
+    width = group_width([block.shape for block, _ in pieces.values()])
+    packed = jnp.concatenate([pack_block(block, width) for block, _ in pieces.values()], axis=0)
+    everything = lax.all_gather(packed, ("row", "col"), axis=0)
+    full = {}
+    start = 0
+    for name, (block, flipped) in pieces.items():
+        height, breadth = block.shape
+        count = height * breadth // width
+        part = unpack_block(everything[:, start : start + count], height, breadth)
+        part = part.reshape(rows, cols, height, breadth)
+        start += count
+        if flipped:
+            full[name] = part.transpose(1, 2, 0, 3).reshape(cols * height, rows * breadth)
+        else:
+            full[name] = part.transpose(0, 2, 1, 3).reshape(rows * height, cols * breadth)
+    return full
+
+
+def scatter_group(pieces, rows, cols):
+    width = group_width([shape for _, shape, _ in pieces.values()])
+    blocks = []
+    for whole, (height, breadth), flipped in pieces.values():
+        whole = whole.astype(jnp.bfloat16)
+        if flipped:
+            part = whole.reshape(cols, height, rows, breadth).transpose(2, 0, 1, 3)
+        else:
+            part = whole.reshape(rows, height, cols, breadth).transpose(0, 2, 1, 3)
+        blocks.append(pack_block(part.reshape(rows * cols, height, breadth), width))
+    packed = jnp.concatenate(blocks, axis=1)
+    total = lax.psum_scatter(packed, ("row", "col"), scatter_dimension=0)
+    mine = {}
+    start = 0
+    for name, (_, (height, breadth), _) in pieces.items():
+        count = height * breadth // width
+        mine[name] = unpack_block(total[start : start + count], height, breadth).astype(
+            jnp.float32
+        )
+        start += count
+    return mine
 
 
 def adam_update(master, moment, second, grad, rate, decay, count):
@@ -291,24 +362,25 @@
     vectors_first,
     vectors_second,
 ):
-    low_embed = embed_weight.astype(jnp.bfloat16)
-    low_enc_wide = encoder_wide_weight.astype(jnp.bfloat16)
-    low_enc_down = encoder_down_weight.astype(jnp.bfloat16)
-    low_dec_wide = decoder_wide_weight.astype(jnp.bfloat16)
-    low_dec_rows = decoder_rows_weight.astype(jnp.bfloat16)
-    across = (
-        lax.all_gather(low_embed, "col", axis=1, tiled=True),
-        lax.all_gather(low_enc_wide, "col", axis=2, tiled=True),
-        lax.all_gather(low_enc_down, "col", axis=2, tiled=True),
-        lax.all_gather(low_dec_wide, "col", axis=1, tiled=True),
-        lax.all_gather(low_dec_rows, "col", axis=1, tiled=True),
-    )
+    rows, cols = lax.axis_size("row"), lax.axis_size("col")
+    low = jnp.bfloat16
+    pieces = {
+        "embed": (embed_weight.astype(low).T, True),
+        "dec_wide": (decoder_wide_weight.astype(low), False),
+        "dec_rows": (decoder_rows_weight.astype(low).T, True),
+    }
+    for depth in range(L):
+        pieces["wide%d" % depth] = (encoder_wide_weight[depth].astype(low), False)
+        pieces["down%d" % depth] = (encoder_down_weight[depth].astype(low).T, True)
+    groups = (("wide0", "down0", "embed"), ("wide1", "down1", "dec_wide", "dec_rows"))
+    order = [name for group in groups for name in group]
+    full = gather_group({name: pieces[name] for name in order}, rows, cols)
     whole = (
-        lax.all_gather(across[0], "row", axis=0, tiled=True),
-        lax.all_gather(across[1], "row", axis=1, tiled=True),
-        lax.all_gather(across[2], "row", axis=1, tiled=True),
-        lax.all_gather(across[3], "row", axis=0, tiled=True),
-        lax.all_gather(across[4], "row", axis=0, tiled=True),
+        full["embed"],
+        tuple(full["wide%d" % depth] for depth in range(L)),
+        tuple(full["down%d" % depth] for depth in range(L)),
+        full["dec_wide"],
+        full["dec_rows"],
     )
     weights = tuple(whole) + (pixel_head_weight.astype(jnp.bfloat16),)
     inverse = 1.0 / (tubes.shape[0] * lax.axis_size("row") * lax.axis_size("col") * NMASK * PIX)
@@ -318,29 +390,25 @@
         value, grads = clip_grads(weights, vectors_weight, tubes[clip], tube_order[clip], inverse)
         loss_local = loss_local + value
         totals = grads if totals is None else jax.tree.map(jnp.add, totals, grads)
-    partial_value = (
-        lax.psum_scatter(
-            totals[0].astype(jnp.bfloat16), "row", scatter_dimension=0, tiled=True
-        ).astype(jnp.float32),
-        lax.psum_scatter(
-            totals[1].astype(jnp.bfloat16), "row", scatter_dimension=1, tiled=True
-        ).astype(jnp.float32),
-        lax.psum_scatter(
-            totals[2].astype(jnp.bfloat16), "row", scatter_dimension=1, tiled=True
-        ).astype(jnp.float32),
-        lax.psum_scatter(
-            totals[3].astype(jnp.bfloat16), "row", scatter_dimension=0, tiled=True
-        ).astype(jnp.float32),
-        lax.psum_scatter(
-            totals[4].astype(jnp.bfloat16), "row", scatter_dimension=0, tiled=True
-        ).astype(jnp.float32),
-    )
+    summed = {"embed": totals[0], "dec_wide": totals[3], "dec_rows": totals[4]}
+    for depth in range(L):
+        summed["wide%d" % depth] = totals[1][depth]
+        summed["down%d" % depth] = totals[2][depth]
+    mine = {}
+    for group in (groups[1], groups[0]):
+        mine.update(
+            scatter_group(
+                {name: (summed[name], pieces[name][0].shape, pieces[name][1]) for name in group},
+                rows,
+                cols,
+            )
+        )
     owned = (
-        lax.psum_scatter(partial_value[0], "col", scatter_dimension=1, tiled=True),
-        lax.psum_scatter(partial_value[1], "col", scatter_dimension=2, tiled=True),
-        lax.psum_scatter(partial_value[2], "col", scatter_dimension=2, tiled=True),
-        lax.psum_scatter(partial_value[3], "col", scatter_dimension=1, tiled=True),
-        lax.psum_scatter(partial_value[4], "col", scatter_dimension=1, tiled=True),
+        mine["embed"].T,
+        jnp.stack([mine["wide%d" % depth] for depth in range(L)]),
+        jnp.stack([mine["down%d" % depth].T for depth in range(L)]),
+        mine["dec_wide"],
+        mine["dec_rows"].T,
     )
     loss, grad_head, grad_vectors = lax.psum((loss_local, totals[5], totals[6]), ("row", "col"))
     grads = tuple(owned) + (grad_head, grad_vectors)

time: 2150 us -> 1780 us (0.83)
  waiting for transfers between devices: 804 us -> 344 us
  local copies, waits for them, and re-layouts: 189 us -> 374 us
  other arithmetic: 349 us -> 296 us
  blocking collectives: 89.6 us -> 39.6 us
    unnamed x21 -> x4, waiting for transfers between devices: 164 us -> 0.07 us
    all_gather x7 -> x1, waiting for transfers between devices: 244 us -> 93.1 us  [gather_group(): everything = lax.all_gather(packed, ('row', 'col'), axis=0)]
    psum x1, waiting for transfers between devices: 87.6 us -> 0.01 us  [shards(): lax.psum((loss_local, totals[5], totals[6]), ('row', 'col'))]
    reshape x0 -> x12, local copies, waits for them, and re-layouts: none -> 69.5 us  [the longest x6 37.9 us: gather_group(): part = part.reshape(rows, cols, height, breadth)]
    reduce_scatter x7 -> x2, waiting for transfers between devices: 309 us -> 251 us  [scatter_group(): total = lax.psum_scatter(packed, ('row', 'col'), scatter_dimension=0)]
    all_gather x3 -> x0, blocking collectives: 49.5 us -> none  [the longest x1 18.8 us: shards(): lax.all_gather(low_embed, 'col', axis=1, tiled=True)]
    transpose x0 -> x8, local copies, waits for them, and re-layouts: none -> 49.4 us  [the longest x4 36.1 us: scatter_group(): part = whole.reshape(rows, height, cols, breadth).transpose(0, 2, 1, 3)]
    another operation x4 -> x2, other arithmetic: 44.1 us -> 1.16 us  [clip_grads(): jnp.stack(wide_grads)]
  transfers between devices with their start and end apart: 18 -> 4, of which waited for: 14 -> 3; matrix products, arithmetic and copies ran while one was open for 18% -> 20% of each run, Pallas kernels for 0% -> 0%
where the time goes in v1:
time: 1780 us; the launch traced here: 1770 us
  matrix products  687 us (39%)
  local copies, waits for them, and re-layouts  374 us (21%)
  waiting for transfers between devices  344 us (19%)
  other arithmetic  296 us (17%)
  blocking collectives  39.6 us (2%)
  between operations  22.5 us (1%)
    reduce_scatter x2, waiting for transfers between devices, scatter_group(): total = lax.psum_scatter(packed, ('row', 'col'), scatter_dimension=0)  251 us
    dot_general x28, matrix products, product(): return jnp.dot(left, right, preferred_element_type=jnp.float32)  155 us
    convert_element_type x8, other arithmetic, attend_back(): grad_scores = (probs * (grad_probs - inner)).astype(jnp.bfloat16)  105 us
    dot_general x8, matrix products, attend_back(): jnp.einsum('qhd,khd->hqk', chosen_grad, values, preferred_element_type=jn...  100 us
    all_gather x1, waiting for transfers between devices, gather_group(): everything = lax.all_gather(packed, ('row', 'col'), axis=0)  93.1 us
    dot_general x30, matrix products, product_left(): lax.dot_general(left, right, (((0,), (0,)), ((), ())), preferred_element_...  91.1 us
    unnamed x939, local copies, waits for them, and re-layouts  85.1 us
    dot_general x30, matrix products, product_right(): lax.dot_general(left, right, (((1,), (1,)), ((), ())), preferred_element_...  78.9 us
  transfers between devices with their start and end apart: 4, of which 3 were waited for; matrix products, arithmetic and copies ran while one was open for 20% of the time, Pallas kernels for 0%

profile of v1, /device:TPU:0, one launch (start us, length us, event | category | flops | bytes accessed | tf_op | source)
XLA Modules:
  0.0 1765.1 jit_solution(11447717387424088823)
XLA Ops:
  82.3 23.8 %gather_fusion.4 = bf16[1411,1536]{1,0:T(8,128)(2,1)} fusion(bf16[1568,1536]{1,0:T(8,128)(2,1)} %get-tuple-element.141, s32[2048]{0:T(1024)S(1)} %pad_clamp_fusion.1), kind=kCustom, calls=%fused_computation.4.clone | custom fusion | bytes 8674828 | tf_op jit(solution)/shard_map/jit(_take)/gather | solution.py:220
  123.6 93.1 %all-gather.4.cloned.1.call-done = bf16[32,708,768]{2,1,0:T(8,128)(2,1)} async-done(((bf16[1,708,768]{2,1,0:T(8,128)(2,1)}), bf16[32,708,768]{2,1,0:T(8,128)(2,1)}) %all-gather.4.cloned.1.call-update) | async-done | bytes 34799632 | tf_op jit(solution)/shard_map/all_gather | solution.py:291
  243.6 15.3 fusion.351
  443.0 14.4 multiply_reduce_fusion.4
  470.9 14.0 fusion.141
  510.5 14.0 fusion.140
  529.8 14.3 multiply_reduce_fusion.6
  557.3 14.0 fusion.139
  616.7 25.0 %multiply_convert_fusion.5 = (bf16[1568,1536]{1,0:T(8,128)(2,1)S(1)}, f32[1568,1536]{1,0:T(8,128)}, f32[1568,1536]{1,0:T(8,128)}) fusion(bf16[384,3072]{1,0:T(8,128)(2,1)S(1)} %bitcast.501, f32[1568,384]{1,0:T(8,128)S(1)} %get-tuple-element.248, f32[384]{0:T(512)S(1)} %copy-done.393, f32[1568]{0:T(1024)S(1)} %fusion.253, f32[1568]{0:T(1024)S(1)} %broadcast_multiply_fusion.6), kind=kOutput, calls=%fused_computation.83 | convolution fusion | flops 2008645632 | bytes 27691008 | tf_op jit(solution)/shard_map/dot_general | solution.py:28
  660.6 24.7 %multiply_convert_fusion.4 = (bf16[1568,1536]{1,0:T(8,128)(2,1)S(1)}, f32[1568,1536]{1,0:T(8,128)}, f32[1568,1536]{1,0:T(8,128)}) fusion(bf16[384,3072]{1,0:T(8,128)(2,1)S(1)} %bitcast.503, f32[1568,384]{1,0:T(8,128)S(1)} %get-tuple-element.273, f32[1568]{0:T(1024)S(1)} %fusion.256, f32[1568]{0:T(1024)S(1)} %broadcast_multiply_fusion.4, f32[384]{0:T(512)S(1)} %copy-done.393), kind=kOutput, calls=%fused_computation.70 | convolution fusion | flops 2008645632 | bytes 27691008 | tf_op jit(solution)/shard_map/dot_general | solution.py:28
  740.0 24.4 %multiply_reduce_fusion.3 = (f32[6,784]{1,0:T(8,128)S(1)}, f32[6,784,1568]{2,1,0:T(8,128)}) fusion(f32[6,784,1568]{2,1,0:T(8,128)} %get-tuple-element.246, f32[6,784]{1,0:T(8,128)S(1)} %copy-done.162, bf16[784,6,64]{0,2,1:T(8,128)(2,1)} %bitcast.477, bf16[1568,6,64]{0,2,1:T(8,128)(2,1)S(1)} %bitcast.463), kind=kOutput, calls=%fused_computation.20 | convolution fusion | flops 973610368 | bytes 60850944 | tf_op jit(solution)/shard_map/qhd,khd->hqk/dot_general | solution.py:109
  764.4 25.7 %multiply_convert_fusion.3 = bf16[6,784,1568]{2,1,0:T(8,128)(2,1)} fusion(f32[6,784,1568]{2,1,0:T(8,128)} %get-tuple-element.284, f32[6,784,1568]{2,1,0:T(8,128)} %get-tuple-element.246, f32[6,784]{1,0:T(8,128)S(1)} %get-tuple-element.283, f32[6,784]{1,0:T(8,128)S(1)} %copy-done.162), kind=kLoop, calls=%fused_computation.19 | loop fusion | flops 36879360 | bytes 73796352 | tf_op jit(solution)/shard_map/convert_element_type | solution.py:113
  812.3 14.2 fusion.14
  826.6 24.8 %multiply_reduce_fusion.2 = (f32[6,784]{1,0:T(8,128)S(1)}, f32[6,784,1568]{2,1,0:T(8,128)}) fusion(f32[6,784,1568]{2,1,0:T(8,128)} %get-tuple-element.244, f32[6,784]{1,0:T(8,128)S(1)} %copy-done.160, bf16[784,6,64]{0,2,1:T(8,128)(2,1)S(1)} %bitcast.482, bf16[1568,6,64]{0,2,1:T(8,128)(2,1)S(1)} %bitcast.464), kind=kOutput, calls=%fused_computation.17 | convolution fusion | flops 973610368 | bytes 60850944 | tf_op jit(solution)/shard_map/qhd,khd->hqk/dot_general | solution.py:109
  854.9 24.1 %multiply_reduce_fusion.1 = (f32[6,784]{1,0:T(8,128)S(1)}, f32[6,784,1568]{2,1,0:T(8,128)}) fusion(f32[6,784,1568]{2,1,0:T(8,128)} %get-tuple-element.271, f32[6,784]{1,0:T(8,128)S(1)} %copy-done.161, bf16[784,6,64]{0,2,1:T(8,128)(2,1)S(1)} %bitcast.479, bf16[1568,6,64]{0,2,1:T(8,128)(2,1)S(1)} %bitcast.459), kind=kOutput, calls=%fused_computation.14 | convolution fusion | flops 973610368 | bytes 60850944 | tf_op jit(solution)/shard_map/qhd,khd->hqk/dot_general | solution.py:109
  879.1 25.6 %multiply_convert_fusion.1 = bf16[6,784,1568]{2,1,0:T(8,128)(2,1)} fusion(f32[6,784,1568]{2,1,0:T(8,128)} %get-tuple-element.280, f32[6,784,1568]{2,1,0:T(8,128)} %get-tuple-element.271, f32[6,784]{1,0:T(8,128)S(1)} %get-tuple-element.279, f32[6,784]{1,0:T(8,128)S(1)} %copy-done.161), kind=kLoop, calls=%fused_computation.13 | loop fusion | flops 36879360 | bytes 73796352 | tf_op jit(solution)/shard_map/convert_element_type | solution.py:113
  940.7 24.2 %multiply_reduce_fusion = (f32[6,784]{1,0:T(8,128)S(1)}, f32[6,784,1568]{2,1,0:T(8,128)}) fusion(f32[6,784,1568]{2,1,0:T(8,128)} %get-tuple-element.269, f32[6,784]{1,0:T(8,128)S(1)} %copy-done.159, bf16[784,6,64]{0,2,1:T(8,128)(2,1)S(1)} %bitcast.484, bf16[1568,6,64]{0,2,1:T(8,128)(2,1)S(1)} %bitcast.460), kind=kOutput, calls=%fused_computation.11 | convolution fusion | flops 973610368 | bytes 60850944 | tf_op jit(solution)/shard_map/qhd,khd->hqk/dot_general | solution.py:109
  964.9 14.0 fusion.68
  992.6 25.6 %multiply_convert_fusion.2 = bf16[6,784,1568]{2,1,0:T(8,128)(2,1)} fusion(f32[6,784,1568]{2,1,0:T(8,128)} %get-tuple-element.286, f32[6,784,1568]{2,1,0:T(8,128)} %get-tuple-element.244, f32[6,784]{1,0:T(8,128)S(1)} %get-tuple-element.285, f32[6,784]{1,0:T(8,128)S(1)} %copy-done.160), kind=kLoop, calls=%fused_computation.16 | loop fusion | flops 36879360 | bytes 73796352 | tf_op jit(solution)/shard_map/convert_element_type | solution.py:113
  1039.2 25.9 %multiply_convert_fusion = bf16[6,784,1568]{2,1,0:T(8,128)(2,1)} fusion(f32[6,784,1568]{2,1,0:T(8,128)} %get-tuple-element.282, f32[6,784,1568]{2,1,0:T(8,128)} %get-tuple-element.269, f32[6,784]{1,0:T(8,128)S(1)} %get-tuple-element.281, f32[6,784]{1,0:T(8,128)S(1)} %copy-done.159), kind=kLoop, calls=%fused_computation.10 | loop fusion | flops 36879360 | bytes 73796352 | tf_op jit(solution)/shard_map/convert_element_type | solution.py:113
  1427.1 14.5 pad_maximum_fusion
  1446.7 39.6 %all-reduce.2 = (f32[]{:T(128)}, f32[5376]{0:T(1024)S(1)}) all-reduce(f32[]{:T(128)S(6)} %multiply.408, f32[5376]{0:T(1024)S(1)} %add.655), channel_id=1, replica_groups=mesh['row'=4,'col'=8] {'row','col'}, use_global_device_ids=true, to_apply=%region_54.60 | all-reduce | flops 5377 | bytes 43016 | tf_op jit(solution)/shard_map/psum | solution.py:413
  1495.1 43.3 %reduce-scatter.3.cloned.1.call-done = bf16[1,336,768]{2,1,0:T(8,128)(2,1)} async-done(((bf16[32,336,768]{2,1,0:T(8,128)(2,1)}), bf16[1,336,768]{2,1,0:T(8,128)(2,1)}) %reduce-scatter.3.cloned.1.call-update) | async-done | bytes 516112 | tf_op jit(solution)/shard_map/reduce_scatter | solution.py:318
  1541.1 207.6 %reduce-scatter.5.cloned.1.call-done = bf16[1,372,768]{2,1,0:T(8,128)(2,1)} async-done(((bf16[32,372,768]{2,1,0:T(8,128)(2,1)}), bf16[1,372,768]{2,1,0:T(8,128)(2,1)}) %reduce-scatter.5.cloned.1.call-update) | async-done | bytes 571408 | tf_op jit(solution)/shard_map/reduce_scatter | solution.py:318
  (1362 shorter events, 956.3 us)
Async XLA Ops:
  7.2 209.5 %all-gather.4.cloned.1.call-start = ((), (), s32[]{:S(2)}) async-start(), calls=%async_computation.5 | async-start | bytes 36089856 | tf_op jit(solution)/shard_map/all_gather | solution.py:291
  12.6 1474.3 %all-reduce.5.cloned.1.call-start = ((), (), s32[]{:S(2)}) async-start(), calls=%async_computation.4 | async-start | bytes 4718592 | tf_op jit(solution)/shard_map/psum | solution.py:413
  82.3 245.7 %copy-start.128 = (bf16[157,1536]{1,0:T(8,128)(2,1)}, bf16[157,1536]{1,0:T(8,128)(2,1)S(1)}, u32[]{:S(2)}) copy-start(bf16[157,1536]{1,0:T(8,128)(2,1)S(1)} %gather_fusion) | copy-start | bytes 1446916
  121.6 266.5 %copy-start.245 = (f32[768]{0:T(1024)}, f32[768]{0:T(1024)S(1)}, u32[]{:S(2)}) copy-start(f32[768]{0:T(1024)S(1)} %get-tuple-element.186) | copy-start | bytes 9220
  121.6 275.1 %copy-start.247 = (f32[768]{0:T(1024)}, f32[768]{0:T(1024)S(1)}, u32[]{:S(2)}) copy-start(f32[768]{0:T(1024)S(1)} %get-tuple-element.185) | copy-start | bytes 9220
  121.6 285.1 %copy-start.242 = (f32[768]{0:T(1024)}, f32[768]{0:T(1024)S(1)}, u32[]{:S(2)}) copy-start(f32[768]{0:T(1024)S(1)} %get-tuple-element.184) | copy-start | bytes 9220
  121.6 293.4 %copy-start.239 = (f32[768]{0:T(1024)}, f32[768]{0:T(1024)S(1)}, u32[]{:S(2)}) copy-start(f32[768]{0:T(1024)S(1)} %get-tuple-element.183) | copy-start | bytes 9220
  123.6 254.0 %copy-start.4 = (f32[1411,384]{1,0:T(8,128)}, f32[1411,384]{1,0:T(8,128)S(1)}, u32[]{:S(2)}) copy-start(f32[1411,384]{1,0:T(8,128)S(1)} %get-tuple-element.222) | copy-start | bytes 6501892
  443.0 67.5 %copy-start.68 = (bf16[1568,384]{0,1:T(8,128)(2,1)}, bf16[1568,384]{0,1:T(8,128)(2,1)S(1)}, u32[]{:S(2)}) copy-start(bf16[1568,384]{0,1:T(8,128)(2,1)S(1)} %copy.230) | copy-start | bytes 3612676
  529.8 67.1 %copy-start.70 = (bf16[1568,384]{0,1:T(8,128)(2,1)}, bf16[1568,384]{0,1:T(8,128)(2,1)S(1)}, u32[]{:S(2)}) copy-start(bf16[1568,384]{0,1:T(8,128)(2,1)S(1)} %copy.218) | copy-start | bytes 3612676
  660.0 72.3 %copy-start.29 = (f32[1568,384]{1,0:T(8,128)}, f32[1568,384]{1,0:T(8,128)S(1)}, u32[]{:S(2)}) copy-start(f32[1568,384]{1,0:T(8,128)S(1)} %get-tuple-element.273) | copy-start | bytes 7225348
  660.0 72.3 %copy-start.279 = (f32[1568]{0:T(1024)}, f32[1568]{0:T(1024)S(1)}, u32[]{:S(2)}) copy-start(f32[1568]{0:T(1024)S(1)} %broadcast_multiply_fusion.4) | copy-start | bytes 18820
  660.6 71.7 %copy-start.308 = (f32[1568]{0:T(1024)}, f32[1568]{0:T(1024)S(1)}, u32[]{:S(2)}) copy-start(f32[1568]{0:T(1024)S(1)} %fusion.256) | copy-start | bytes 18820
  713.7 137.7 %copy-start.36 = (f32[1411,384]{1,0:T(8,128)}, f32[1411,384]{1,0:T(8,128)S(1)}, u32[]{:S(2)}) copy-start(f32[1411,384]{1,0:T(8,128)S(1)} %broadcast_add_fusion) | copy-start | bytes 6501892
  1207.6 330.8 %reduce-scatter.3.cloned.1.call-start = ((), (), s32[]{:S(2)}) async-start(), calls=%async_computation.2 | async-start | bytes 17031168 | tf_op jit(solution)/shard_map/reduce_scatter | solution.py:318
  1306.0 442.8 %reduce-scatter.5.cloned.1.call-start = ((), (), s32[]{:S(2)}) async-start(), calls=%async_computation.3 | async-start | bytes 19058688 | tf_op jit(solution)/shard_map/reduce_scatter | solution.py:318
  1495.0 255.6 %copy-start.238 = (f32[576,48]{0,1:T(8,128)S(1)}, f32[576,48]{0,1:T(8,128)}, u32[]{:S(2)}) copy-start(f32[576,48]{0,1:T(8,128)} %param.49) | copy-start | bytes 331780
  1495.0 255.6 %copy-start.265 = (f32[576,48]{0,1:T(8,128)S(1)}, f32[576,48]{0,1:T(8,128)}, u32[]{:S(2)}) copy-start(f32[576,48]{0,1:T(8,128)} %param.51) | copy-start | bytes 331780
  1495.0 257.3 %copy-start.234 = (f32[96,384]{1,0:T(8,128)S(1)}, f32[96,384]{1,0:T(8,128)}, u32[]{:S(2)}) copy-start(f32[96,384]{1,0:T(8,128)} %param.46) | copy-start | bytes 442372
  1495.0 257.3 %copy-start.255 = (f32[96,384]{1,0:T(8,128)S(1)}, f32[96,384]{1,0:T(8,128)}, u32[]{:S(2)}) copy-start(f32[96,384]{1,0:T(8,128)} %param.48) | copy-start | bytes 442372
  1495.1 257.3 %copy-start.256 = (f32[96,384]{1,0:T(8,128)S(1)}, f32[96,384]{1,0:T(8,128)}, u32[]{:S(2)}) copy-start(f32[96,384]{1,0:T(8,128)} %param.47) | copy-start | bytes 442372
  1495.1 258.2 %copy-start.168 = (f32[2,768,96]{1,2,0:T(8,128)S(1)}, f32[2,768,96]{1,2,0:T(8,128)}, u32[]{:S(2)}) copy-start(f32[2,768,96]{1,2,0:T(8,128)} %param.43) | copy-start | bytes 1769476
  1495.1 258.2 %copy-start.235 = (f32[2,768,96]{1,2,0:T(8,128)S(1)}, f32[2,768,96]{1,2,0:T(8,128)}, u32[]{:S(2)}) copy-start(f32[2,768,96]{1,2,0:T(8,128)} %param.45) | copy-start | bytes 1769476
  1495.1 258.2 %copy-start.236 = (f32[2,768,96]{1,2,0:T(8,128)S(1)}, f32[2,768,96]{1,2,0:T(8,128)}, u32[]{:S(2)}) copy-start(f32[2,768,96]{1,2,0:T(8,128)} %param.44) | copy-start | bytes 1769476
  (437 other events, 2607.4 us)
Sparse Core Ops, SparseCore 0:
  12.7 203.9 all-gather.3
  1207.7 133.7 all-reduce.4
  1347.9 190.4 reduce-scatter.2
  1544.7 203.9 reduce-scatter.4

commit v2 on v1

v2 whole, which is shorter than its diff:
```python
import jax
import jax.numpy as jnp
from jax import lax
from jax.experimental import pallas as pl
from jax.experimental.pallas import tpu as pltpu
from jax.sharding import PartitionSpec as P

D = 768
HEADS = 12
HDIM = 64
FF = 3072
DD = 384
DHEADS = 6
DFF = 1536
PIX = 1536
L = 2
NTUBE = 1568
NVIS = 157
NMASK = 1411
NPAD = 160
PAIR = 2 * HDIM


beta_first = 0.5
beta_second = 0.5
adam_epsilon = 1e-08
decay_factor = 0.05
norm_epsilon = 1e-06


def product(left, right):
    return jnp.dot(left, right, preferred_element_type=jnp.float32)


def product_left(left, right):
    return lax.dot_general(
        left, right, (((0,), (0,)), ((), ())), preferred_element_type=jnp.float32
    )


def product_right(left, right):
    return lax.dot_general(
        left, right, (((1,), (1,)), ((), ())), preferred_element_type=jnp.float32
    )


def sinusoid(places, width):
    columns = jnp.arange(width // 2, dtype=jnp.float32)[None, :]
    angles = places[:, None] * jnp.exp(columns * (-2.0 * jnp.log(10000.0) / width))
    return jnp.concatenate([jnp.sin(angles), jnp.cos(angles)], axis=1)


def layer_norm(values, gain):
    average = jnp.mean(values, axis=-1, keepdims=True)
    centred = values - average
    spread = jnp.mean(centred * centred, axis=-1, keepdims=True)
    return centred * lax.rsqrt(spread + norm_epsilon) * gain


def gelu_parts(values):
    below = 0.5 * (1.0 + lax.erf(values * 0.5**0.5))
    density = jnp.exp(-0.5 * values * values) * (2.0 * jnp.pi) ** (-0.5)
    return (values * below, below + values * density)


def contract(left, right, left_dim, right_dim):
    return lax.dot_general(
        left,
        right,
        (((left_dim,), (right_dim,)), ((), ())),
        preferred_element_type=jnp.float32,
    )


def lane_halves(shape):
    lane = lax.broadcasted_iota(jnp.int32, shape, 1)
    return (lane < HDIM, lane >= HDIM)


def attend_kernel(valid, q_ref, k_ref, v_ref, o_ref, t_ref):
    queries = q_ref[...] * jnp.bfloat16(HDIM**-0.5)
    halves = lane_halves(queries.shape)
    keys = k_ref[...]
    values = v_ref[...]
    outputs = []
    totals = []
    for half in halves:
        chosen = jnp.where(half, queries, jnp.bfloat16(0))
        scores = contract(chosen, keys, 1, 1)
        if valid < keys.shape[0]:
            known = lax.broadcasted_iota(jnp.int32, scores.shape, 1) < valid
            scores = jnp.where(known, scores, -3e38)
        largest = jnp.max(scores, axis=1, keepdims=True)
        raised = jnp.exp(scores - largest)
        summed = jnp.sum(raised, axis=1, keepdims=True)
        outputs.append(contract(raised.astype(jnp.bfloat16), values, 1, 0) / summed)
        totals.append(largest + jnp.log(summed))
    o_ref[...] = jnp.where(halves[0], outputs[0], outputs[1]).astype(jnp.bfloat16)
    t_ref[...] = jnp.where(halves[0], totals[0], totals[1])


def attend_back_kernel(
    valid, q_ref, k_ref, v_ref, t_ref, g_ref, dq_ref, dk_ref, dv_ref, ak_ref, av_ref
):
    step = pl.program_id(2)

    @pl.when(step == 0)
    def _():
        ak_ref[...] = jnp.zeros_like(ak_ref)
        av_ref[...] = jnp.zeros_like(av_ref)

    queries = q_ref[...] * jnp.bfloat16(HDIM**-0.5)
    keys = k_ref[...]
    values = v_ref[...]
    grads = g_ref[...]
    totals = t_ref[...]
    halves = lane_halves(queries.shape)
    parts = []
    for index, half in enumerate(halves):
        chosen = jnp.where(half, queries, jnp.bfloat16(0))
        grad = jnp.where(half, grads, jnp.bfloat16(0))
        scores = contract(chosen, keys, 1, 1)
        if valid < keys.shape[0]:
            known = lax.broadcasted_iota(jnp.int32, scores.shape, 1) < valid
            scores = jnp.where(known, scores, -3e38)
        probs = jnp.exp(scores - totals[:, index * HDIM : index * HDIM + 1])
        lifted = probs * contract(grad, values, 1, 1)
        inner = jnp.sum(lifted, axis=1, keepdims=True)
        grad_scores = (lifted - probs * inner).astype(jnp.bfloat16)
        parts.append(contract(grad_scores, keys, 1, 0))
        ak_ref[...] += contract(grad_scores, chosen, 0, 0)
        av_ref[...] += contract(probs.astype(jnp.bfloat16), grad, 0, 0)
    mixed = jnp.where(halves[0], parts[0], parts[1]) * HDIM ** (-0.5)
    dq_ref[...] = mixed.astype(jnp.bfloat16)

    @pl.when(step == pl.num_programs(2) - 1)
    def _():
        dk_ref[...] = ak_ref[...].astype(jnp.bfloat16)
        dv_ref[...] = av_ref[...].astype(jnp.bfloat16)


def attend(packed, clips, heads, valid, block):
    length = packed.shape[0] // clips
    pairs = heads // 2
    steps = length // block
    some = pl.BlockSpec((block, PAIR), lambda c, h, i: (c * steps + i, h))
    tall = packed.shape[0]
    return pl.pallas_call(
        lambda *refs: attend_kernel(valid, *refs),
        grid=(clips, pairs, steps),
        in_specs=[
            some,
            pl.BlockSpec((length, PAIR), lambda c, h, i: (c, pairs + h)),
            pl.BlockSpec((length, PAIR), lambda c, h, i: (c, 2 * pairs + h)),
        ],
        out_specs=[some, some],
        out_shape=[
            jax.ShapeDtypeStruct((tall, heads * HDIM), jnp.bfloat16),
            jax.ShapeDtypeStruct((tall, heads * HDIM), jnp.float32),
        ],
        cost_estimate=pl.CostEstimate(
            flops=16 * tall * length * heads * HDIM,
            bytes_accessed=12 * tall * heads * HDIM,
            transcendentals=tall * length * heads,
        ),
        name="attend",
    )(packed, packed, packed)


def attend_back(packed, totals, grads, clips, heads, valid, block):
    length = packed.shape[0] // clips
    pairs = heads // 2
    steps = length // block
    some = pl.BlockSpec((block, PAIR), lambda c, h, i: (c * steps + i, h))
    every = pl.BlockSpec((length, PAIR), lambda c, h, i: (c, h))
    tall = packed.shape[0]
    shape = jax.ShapeDtypeStruct((tall, heads * HDIM), jnp.bfloat16)
    return pl.pallas_call(
        lambda *refs: attend_back_kernel(valid, *refs),
        grid=(clips, pairs, steps),
        in_specs=[
            some,
            pl.BlockSpec((length, PAIR), lambda c, h, i: (c, pairs + h)),
            pl.BlockSpec((length, PAIR), lambda c, h, i: (c, 2 * pairs + h)),
            some,
            some,
        ],
        out_specs=[some, every, every],
        out_shape=[shape, shape, shape],
        scratch_shapes=[
            pltpu.VMEM((length, PAIR), jnp.float32),
            pltpu.VMEM((length, PAIR), jnp.float32),
        ],
        cost_estimate=pl.CostEstimate(
            flops=40 * tall * length * heads * HDIM,
            bytes_accessed=20 * tall * heads * HDIM,
            transcendentals=tall * length * heads,
        ),
        name="attend_back",
    )(packed, packed, packed, totals, grads)


def layer_forward(stream, wide, down, gain_first, gain_second, form):
    width = stream.shape[1]
    normed, back_first = jax.vjp(layer_norm, stream, gain_first)
    normed = normed.astype(jnp.bfloat16)
    packed = product(normed, wide[:, : 3 * width]).astype(jnp.bfloat16)
    mixed, totals = attend(packed, *form)
    middle = stream + product(mixed, wide[:, 3 * width : 4 * width])
    second, back_second = jax.vjp(layer_norm, middle, gain_second)
    second = second.astype(jnp.bfloat16)
    activated, slope = gelu_parts(product(second, wide[:, 4 * width :]))
    activated = activated.astype(jnp.bfloat16)
    slope = slope.astype(jnp.bfloat16)
    output = middle + product_right(activated, down)
    return (
        output,
        (back_first, normed, packed, mixed, totals, back_second, second, slope, activated),
    )


def layer_backward(grad_stream, wide, down, kept, form):
    back_first, normed, packed, mixed, totals, back_second, second, slope, activated = kept
    low = jnp.bfloat16
    width = grad_stream.shape[1]
    grad_branch = grad_stream.astype(low)
    grad_down = product_left(grad_branch, activated).astype(low)
    grad_hidden = (slope.astype(jnp.float32) * product(grad_branch, down)).astype(low)
    grad_up = product_left(second, grad_hidden).astype(low)
    grad_middle, grad_gain_second = back_second(product_right(grad_hidden, wide[:, 4 * width :]))
    grad_middle = grad_stream + grad_middle
    grad_attend = grad_middle.astype(low)
    grad_output = product_left(mixed, grad_attend).astype(low)
    grad_mixed = product_right(grad_attend, wide[:, 3 * width : 4 * width]).astype(low)
    grad_parts = attend_back(packed, totals, grad_mixed, *form)
    grad_packed = jnp.concatenate(grad_parts, axis=1)
    grad_qkv = product_left(normed, grad_packed).astype(low)
    grad_before, grad_gain_first = back_first(product_right(grad_packed, wide[:, : 3 * width]))
    grad_wide = (grad_qkv, grad_output, grad_up)
    return (grad_middle + grad_before, grad_wide, grad_down, grad_gain_first, grad_gain_second)


def all_grads(weights, head, vectors, tubes, orders, inverse, reduce_head, reduce_late):
    clips = tubes.shape[0]
    low = jnp.bfloat16
    base = (2 * L + 1) * D
    encoder_form = (clips, HEADS, NVIS, NPAD)
    decoder_form = (clips, DHEADS, NTUBE, NTUBE // 7)
    visible = jnp.pad(orders[:, :NVIS], ((0, 0), (0, NPAD - NVIS)), constant_values=-1)
    chosen = visible[:, :, None] == jnp.arange(NTUBE, dtype=jnp.int32)[None, None, :]
    chosen_low = chosen.astype(low)
    shown = jnp.any(chosen, axis=1)
    pixels = tubes.reshape(clips * NTUBE, PIX)
    seen = jnp.einsum("cvp,cpd->cvd", chosen_low, tubes, preferred_element_type=jnp.float32)
    seen = seen.astype(low).reshape(clips * NPAD, PIX)
    places = visible.reshape(-1).astype(jnp.float32)
    stream = product_right(seen, weights["embed"]) + sinusoid(places, D)
    kept_layers = []
    for depth in range(L):
        stream, kept = layer_forward(
            stream,
            weights["wide%d" % depth],
            weights["down%d" % depth],
            vectors[2 * depth * D : (2 * depth + 1) * D],
            vectors[(2 * depth + 1) * D : (2 * depth + 2) * D],
            encoder_form,
        )
        kept_layers.append(kept)
    normed, back_encoder = jax.vjp(layer_norm, stream, vectors[2 * L * D : base])
    normed = normed.astype(low)
    bridge = weights["dec_rows"][:, DFF:]
    bridged = product_right(normed, bridge).reshape(clips, NPAD, DD)
    placed = jnp.einsum(
        "cvp,cvd->cpd",
        chosen.astype(jnp.float32),
        bridged,
        precision=lax.Precision.HIGHEST,
        preferred_element_type=jnp.float32,
    )
    token_mask = vectors[base + 3 * DD : base + 4 * DD]
    table = sinusoid(jnp.arange(NTUBE, dtype=jnp.float32), DD)
    decoded = jnp.where(shown[:, :, None], placed, token_mask) + table[None]
    decoded = decoded.reshape(clips * NTUBE, DD)
    hidden_rows = jnp.logical_not(shown).reshape(-1, 1)
    decoded, kept_decoder = layer_forward(
        decoded,
        weights["dec_wide"],
        weights["dec_rows"][:, :DFF],
        vectors[base : base + DD],
        vectors[base + DD : base + 2 * DD],
        decoder_form,
    )
    final, back_final = jax.vjp(layer_norm, decoded, vectors[base + 2 * DD : base + 3 * DD])
    final = final.astype(low)
    target = layer_norm(pixels.astype(jnp.float32), 1.0)
    error = jnp.where(hidden_rows, product(final, head) - target, 0.0)
    loss_value = jnp.sum(error * error) * inverse
    grad_predicted = (2.0 * inverse * error).astype(low)
    grad_head = reduce_head(product_left(final, grad_predicted))
    grad_decoded, grad_gain_final = back_final(product_right(grad_predicted, head))
    grads = {}
    grad_decoded, grads["dec_wide"], grad_dec_down, dec_gain_first, dec_gain_second = (
        layer_backward(
            grad_decoded,
            weights["dec_wide"],
            weights["dec_rows"][:, :DFF],
            kept_decoder,
            decoder_form,
        )
    )
    grads["dec_wide"] = jnp.concatenate(grads["dec_wide"], axis=1)
    grad_decoded, grad_head = lax.optimization_barrier((grad_decoded, grad_head))
    grad_token = jnp.sum(jnp.where(hidden_rows, grad_decoded, 0.0), axis=0)
    grad_bridged = jnp.einsum(
        "cvp,cpd->cvd",
        chosen_low,
        grad_decoded.astype(low).reshape(clips, NTUBE, DD),
        preferred_element_type=jnp.float32,
    )
    grad_bridged = grad_bridged.astype(low).reshape(clips * NPAD, DD)
    grad_bridge = product_left(grad_bridged, normed).astype(low)
    grads["dec_rows"] = jnp.concatenate([grad_dec_down, grad_bridge], axis=1)
    grad_stream, grad_gain_encoder = back_encoder(product(grad_bridged, bridge))
    gain_grads = [None] * L
    mine = {}
    for depth in reversed(range(L)):
        grad_stream, grads["wide%d" % depth], grads["down%d" % depth], first_gain, second_gain = (
            layer_backward(
                grad_stream,
                weights["wide%d" % depth],
                weights["down%d" % depth],
                kept_layers[depth],
                encoder_form,
            )
        )
        gain_grads[depth] = jnp.concatenate([first_gain, second_gain])
        if depth == 0:
            grads["embed"] = product_left(grad_stream.astype(low), seen).astype(low)
        mine.update(reduce_late(grads, depth))
    grad_vectors = jnp.concatenate(
        gain_grads
        + [grad_gain_encoder, dec_gain_first, dec_gain_second, grad_gain_final, grad_token]
    )
    return (loss_value, mine, grad_head, grad_vectors)


BOTH = ("row", "col")


def exchange(value, bit):
    return lax.ppermute(value, BOTH, [(i, i ^ bit) for i in range(32)])


def rotate(value):
    return lax.ppermute(value, BOTH, [(i, (i & ~6) | ((i + 2) & 6)) for i in range(32)])


def own_place():
    row, col = lax.axis_index("row"), lax.axis_index("col")
    return {"y": row // 2, "x": row % 2, "z": col // 2, "c": col % 2}


BITS = {"y": 16, "x": 8, "c": 1}
GATHER_NAMES = ("yxcz", "xczy", "zcyx")
SCATTER_NAMES = ("cyxz", "cxzy", "czyx")
EXTENT = {"y": 2, "x": 2, "z": 4, "c": 2}


def set_block(total, block, start):
    return lax.dynamic_update_slice(total, block, (start, 0, 0))


def ordered_pair(own, name, place):
    other = exchange(own, BITS[name])
    first = place[name] == 0
    return jnp.concatenate([jnp.where(first, own, other), jnp.where(first, other, own)], axis=0)


def ring_blocks(own):
    blocks = [own]
    for _ in range(3):
        blocks.append(rotate(blocks[-1]))
    return blocks


def ring_gather(own, place):
    count = own.shape[0]
    total = jnp.zeros((4 * count,) + own.shape[1:], own.dtype)
    for hop, block in enumerate(ring_blocks(own)):
        total = set_block(total, block, (place["z"] - hop) % 4 * count)
    return total


def gather_chunk(own, form, place):
    own = own[None]
    y, x, z, c = (place[name] for name in "yxzc")
    if form == 0:
        near = ring_gather(own, place)
        aside = exchange(near, BITS["x"])
        found = [(y * 2 + x, near), (y * 2 + 1 - x, aside)]
        found.append(((1 - y) * 2 + x, exchange(near, BITS["y"])))
        found.append(((1 - y) * 2 + 1 - x, exchange(aside, BITS["y"])))
    elif form == 1:
        near = ring_gather(ordered_pair(own, "y", place), place)
        found = [(x, near), (1 - x, exchange(near, BITS["x"]))]
    else:
        near = ordered_pair(ordered_pair(own, "x", place), "y", place)
        found = [((z - hop) % 4, block) for hop, block in enumerate(ring_blocks(near))]
    count = near.shape[0]
    total = jnp.zeros((32,) + own.shape[1:], own.dtype)
    for at, block in found:
        total = set_block(total, block, (at * 2 + c) * count)
        total = set_block(total, exchange(block, BITS["c"]), (at * 2 + 1 - c) * count)
    return total


def take_block(value, index, parts):
    count = value.shape[0] // parts
    return lax.dynamic_slice_in_dim(value, index * count, count, 0)


def reduce_pair(value, name, place):
    sent = take_block(value, 1 - place[name], 2).astype(jnp.bfloat16)
    kept = take_block(value, place[name], 2).astype(jnp.float32)
    return kept + exchange(sent, BITS[name]).astype(jnp.float32)


def ring_reduce(value, place):
    z = place["z"]
    total = take_block(value, (z + 3) % 4, 4)
    for hop in range(1, 4):
        moved = rotate(total.astype(jnp.bfloat16)).astype(jnp.float32)
        total = moved + take_block(value, (z + 3 - hop) % 4, 4).astype(jnp.float32)
    return total


def scatter_chunk(value, form, place):
    for name in SCATTER_NAMES[form]:
        value = ring_reduce(value, place) if name == "z" else reduce_pair(value, name, place)
    return value[0]


def sum_small(value):
    for bit in (1, 2, 4, 8, 16):
        value = value + exchange(value, bit)
    return value


def pack_block(block, width):
    height, breadth = block.shape[-2:]
    lead = block.shape[:-2]
    if breadth == width:
        return block
    if width % breadth == 0 and height % (width // breadth) == 0:
        times = width // breadth
        each = height // times
        return jnp.concatenate(
            [block[..., part * each : (part + 1) * each, :] for part in range(times)], axis=-1
        )
    return block.reshape(lead + (height * breadth // width, width))


def unpack_block(block, height, breadth):
    width = block.shape[-1]
    lead = block.shape[:-2]
    if breadth == width:
        return block
    if width % breadth == 0 and height % (width // breadth) == 0:
        times = width // breadth
        return jnp.concatenate(
            [block[..., part * breadth : (part + 1) * breadth] for part in range(times)], axis=-2
        )
    return block.reshape(lead + (height, breadth))


def slot_of(names, step):
    col = step % 8
    row = step // 8
    index = {"y": row // 2, "x": row % 2, "z": col // 2, "c": col % 2}
    slot = 0
    for name in names:
        slot = slot * EXTENT[name] + index[name]
    return slot


def unpack_kernel(layout, from_ref, *to_refs):
    start = 0
    for to_ref, halves in zip(to_refs, layout):
        if halves is None:
            count = to_ref.shape[1]
            to_ref[0] = from_ref[0, start : start + count, :]
        elif halves == 1:
            count = to_ref.shape[0]
            to_ref[...] = from_ref[0, start : start + count, :]
        else:
            count = to_ref.shape[0] // 2
            breadth = to_ref.shape[1]
            to_ref[:count, :] = from_ref[0, start : start + count, :breadth]
            to_ref[count:, :] = from_ref[0, start : start + count, breadth:]
        start += count


def whole_spec(height, breadth, parts=None):
    first, last = parts or (0, 7)
    return pl.BlockSpec(
        (height, breadth),
        lambda step: (step // 8, jnp.clip(step % 8 - first, 0, last - first)),
    )


def flipped_spec(height, breadth):
    return pl.BlockSpec((height, breadth), lambda step: (step % 8, step // 8))


def halves_of(shape):
    if shape[1] == PACKED:
        return 1
    return 2 if 2 * shape[1] == PACKED else None


def unpack_chunk(total, form, pieces, chunk):
    names = GATHER_NAMES[form]
    layout = []
    specs = []
    shapes = []
    for name in chunk:
        block, flipped = pieces[name]
        height, breadth = block.shape
        halves = halves_of(block.shape)
        layout.append(halves)
        if halves is None:
            count = height * breadth // PACKED
            specs.append(pl.BlockSpec((1, count, PACKED), lambda step: (step, 0, 0)))
            shapes.append(jax.ShapeDtypeStruct((32, count, PACKED), block.dtype))
        elif flipped:
            specs.append(flipped_spec(height, breadth))
            shapes.append(jax.ShapeDtypeStruct((8 * height, 4 * breadth), block.dtype))
        else:
            specs.append(whole_spec(height, breadth))
            shapes.append(jax.ShapeDtypeStruct((4 * height, 8 * breadth), block.dtype))
    found = pl.pallas_call(
        lambda *refs: unpack_kernel(layout, *refs),
        grid=(32,),
        in_specs=[
            pl.BlockSpec((1,) + total.shape[1:], lambda step: (slot_of(names, step), 0, 0))
        ],
        out_specs=specs,
        out_shape=shapes,
        cost_estimate=pl.CostEstimate(
            flops=0, bytes_accessed=4 * total.size, transcendentals=0
        ),
        name="unpack_chunk",
    )(total)
    full = {}
    for name, value, halves in zip(chunk, found, layout):
        if halves is None:
            block, flipped = pieces[name]
            height, breadth = block.shape
            value = value.reshape(4, 8, height, breadth).transpose(1, 2, 0, 3)
            value = value.reshape(8 * height, 4 * breadth)
        full[name] = value
    return full


def pack_kernel(split, halves, refs, outs):
    step = pl.program_id(0)
    col = step % 8
    qkv_ref, out_ref, up_ref, down_ref, small_ref = refs[:5]
    top, side, deep = outs
    for part_ref, first, last in ((qkv_ref, 0, 2), (out_ref, 3, 3), (up_ref, 4, 7)):

        @pl.when(jnp.logical_and(col >= first, col <= last))
        def _():
            top[0] = part_ref[:split, :]
            rest = part_ref.shape[0] - split
            side[0, :rest, :] = part_ref[split:, :]

    rest = qkv_ref.shape[0] - split
    count = small_ref.shape[0] // 2
    breadth = small_ref.shape[1]
    side[0, rest : rest + count, :breadth] = small_ref[:count, :]
    side[0, rest : rest + count, breadth:] = small_ref[count:, :]
    if len(refs) > 5:
        side[0, rest + count :, :] = refs[5][0]
    deep[0] = down_ref[...]


def pack_chunks(grads, pieces, depth):
    wide = pieces["wide%d" % depth][0].shape
    down = pieces["down%d" % depth][0].shape
    small = "dec_wide" if depth else "embed"
    height, breadth = pieces[small][0].shape
    args = list(grads["wide%d" % depth]) + [grads["down%d" % depth], grads[small]]
    specs = [whole_spec(*wide, parts=parts) for parts in ((0, 2), (3, 3), (4, 7))]
    specs.append(flipped_spec(*down))
    specs.append((flipped_spec if pieces[small][1] else whole_spec)(height, breadth))
    side = wide[0] - SPLIT + height // 2
    if depth:
        tall, broad = pieces["dec_rows"][0].shape
        count = tall * broad // PACKED
        value = grads["dec_rows"].reshape(8, tall, 4, broad).transpose(2, 0, 1, 3)
        args.append(value.reshape(32, count, PACKED))
        specs.append(pl.BlockSpec((1, count, PACKED), lambda step: (step, 0, 0)))
        side += count
    counts = (SPLIT, side, down[0])
    number = len(args)
    return pl.pallas_call(
        lambda *refs: pack_kernel(SPLIT, 2, refs[:number], refs[number:]),
        grid=(32,),
        in_specs=specs,
        out_specs=[
            pl.BlockSpec(
                (1, count, PACKED), lambda step, names=names: (slot_of(names, step), 0, 0)
            )
            for count, names in zip(counts, SCATTER_NAMES)
        ],
        out_shape=[jax.ShapeDtypeStruct((32, count, PACKED), jnp.bfloat16) for count in counts],
        cost_estimate=pl.CostEstimate(
            flops=0, bytes_accessed=128 * sum(counts) * PACKED, transcendentals=0
        ),
        name="pack_chunks",
    )(*args)


PACKED = 768
GATHER_CHUNKS = (("wide0", "embed", "dec_rows"), ("wide1", "dec_wide"), ("down0", "down1"))
SPLIT = 144
SCATTER_NAMES_OF = {1: ("wide1", "down1", "dec_wide", "dec_rows"), 0: ("wide0", "down0", "embed")}


def gather_near(pieces, place):
    full = {}
    for form, chunk in enumerate(GATHER_CHUNKS):
        own = jnp.concatenate([pack_block(pieces[name][0], PACKED) for name in chunk], axis=0)
        total = gather_chunk(own, form, place)
        full.update(unpack_chunk(total, form, pieces, chunk))
    return full


def scatter_near(grads, pieces, depth, place):
    top, side, deep = (
        scatter_chunk(value, form, place)
        for form, value in enumerate(pack_chunks(grads, pieces, depth))
    )
    rest = pieces["wide%d" % depth][0].shape[0] - SPLIT
    small = "dec_wide" if depth else "embed"
    height, breadth = pieces[small][0].shape
    mine = {
        "wide%d" % depth: jnp.concatenate([top, side[:rest]], axis=0),
        "down%d" % depth: deep,
        small: unpack_block(side[rest : rest + height // 2], height, breadth),
    }
    if depth:
        shape = pieces["dec_rows"][0].shape
        mine["dec_rows"] = side[rest + height // 2 :].reshape(shape)
    return mine


def gather_far(pieces):
    full = {}
    for name, (block, flipped) in pieces.items():
        first, second = ("col", "row") if flipped else ("row", "col")
        across = lax.all_gather(block, second, axis=1, tiled=True)
        full[name] = lax.all_gather(across, first, axis=0, tiled=True)
    return full


def scatter_far(grads, pieces, names):
    mine = {}
    for name in names:
        if name.startswith("wide"):
            grads = dict(grads, **{name: jnp.concatenate(grads[name], axis=1)})
        row_dim = 1 if pieces[name][1] else 0
        part = lax.psum_scatter(grads[name], "row", scatter_dimension=row_dim, tiled=True)
        mine[name] = lax.psum_scatter(
            part.astype(jnp.float32), "col", scatter_dimension=1 - row_dim, tiled=True
        )
    return mine


def adam_update(master, moment, second, grad, rate, decay, count):
    moment = beta_first * moment + (1.0 - beta_first) * grad
    second = beta_second * second + (1.0 - beta_second) * grad * grad
    first_hat = moment / (1.0 - beta_first**count)
    second_hat = second / (1.0 - beta_second**count)
    master = master - rate * (first_hat / (jnp.sqrt(second_hat) + adam_epsilon) + decay * master)
    return (master, moment, second)


def shards(
    tubes,
    tube_order,
    step_count,
    embed_weight,
    embed_first,
    embed_second,
    encoder_wide_weight,
    encoder_wide_first,
    encoder_wide_second,
    encoder_down_weight,
    encoder_down_first,
    encoder_down_second,
    decoder_wide_weight,
    decoder_wide_first,
    decoder_wide_second,
    decoder_rows_weight,
    decoder_rows_first,
    decoder_rows_second,
    pixel_head_weight,
    pixel_head_first,
    pixel_head_second,
    vectors_weight,
    vectors_first,
    vectors_second,
):
    low = jnp.bfloat16
    pieces = {
        "embed": (embed_weight.astype(low).T, True),
        "dec_wide": (decoder_wide_weight.astype(low), False),
        "dec_rows": (decoder_rows_weight.astype(low).T, True),
    }
    for depth in range(L):
        pieces["wide%d" % depth] = (encoder_wide_weight[depth].astype(low), False)
        pieces["down%d" % depth] = (encoder_down_weight[depth].astype(low).T, True)
    near = (lax.axis_size("row"), lax.axis_size("col")) == (4, 8)
    place = own_place() if near else None
    weights = gather_near(pieces, place) if near else gather_far(pieces)

    def reduce_head(grad):
        return lax.psum(grad, BOTH)

    def reduce_late(grads, depth):
        if near:
            return scatter_near(grads, pieces, depth, place)
        return scatter_far(grads, pieces, SCATTER_NAMES_OF[depth])

    inverse = 1.0 / (tubes.shape[0] * lax.axis_size("row") * lax.axis_size("col") * NMASK * PIX)
    loss_local, mine, grad_head, grad_vectors = all_grads(
        weights,
        pixel_head_weight.astype(low),
        vectors_weight,
        tubes,
        tube_order,
        inverse,
        reduce_head,
        reduce_late,
    )
    small = jnp.concatenate([loss_local[None], grad_vectors])
    small = sum_small(small) if near else lax.psum(small, BOTH)
    loss = small[0]
    grads = (
        mine["embed"].T,
        jnp.stack([mine["wide%d" % depth] for depth in range(L)]),
        jnp.stack([mine["down%d" % depth].T for depth in range(L)]),
        mine["dec_wide"],
        mine["dec_rows"].T,
        grad_head,
        small[1:],
    )
    masters = (
        embed_weight,
        encoder_wide_weight,
        encoder_down_weight,
        decoder_wide_weight,
        decoder_rows_weight,
        pixel_head_weight,
        vectors_weight,
    )
    firsts = (
        embed_first,
        encoder_wide_first,
        encoder_down_first,
        decoder_wide_first,
        decoder_rows_first,
        pixel_head_first,
        vectors_first,
    )
    seconds = (
        embed_second,
        encoder_wide_second,
        encoder_down_second,
        decoder_wide_second,
        decoder_rows_second,
        pixel_head_second,
        vectors_second,
    )
    count = step_count[0].astype(jnp.float32)
    rates = (
        PIX ** (-0.5),
        D ** (-0.5),
        FF ** (-0.5),
        DD ** (-0.5),
        DFF ** (-0.5),
        DD ** (-0.5),
        0.1,
    )
    decays = (decay_factor,) * 6 + (0.0,)
    results = [loss]
    for index in range(7):
        results.extend(
            adam_update(
                masters[index],
                firsts[index],
                seconds[index],
                grads[index],
                rates[index],
                decays[index],
                count,
            )
        )
    return tuple(results)


def solution(mesh):
    placed = (
        P(("row", "col"), None, None),
        P(("row", "col"), None),
        P(),
        P("row", "col"),
        P("row", "col"),
        P("row", "col"),
        P(None, "row", "col"),
        P(None, "row", "col"),
        P(None, "row", "col"),
        P(None, "row", "col"),
        P(None, "row", "col"),
        P(None, "row", "col"),
        P("row", "col"),
        P("row", "col"),
        P("row", "col"),
        P("row", "col"),
        P("row", "col"),
        P("row", "col"),
        P(),
        P(),
        P(),
        P(),
        P(),
        P(),
    )
    return jax.shard_map(
        shards,
        mesh=mesh,
        in_specs=placed,
        out_specs=(
            P(),
            P("row", "col"),
            P("row", "col"),
            P("row", "col"),
            P(None, "row", "col"),
            P(None, "row", "col"),
            P(None, "row", "col"),
            P(None, "row", "col"),
            P(None, "row", "col"),
            P(None, "row", "col"),
            P("row", "col"),
            P("row", "col"),
            P("row", "col"),
            P("row", "col"),
            P("row", "col"),
            P("row", "col"),
            P(),
            P(),
            P(),
            P(),
            P(),
            P(),
        ),
        check_vma=False,
    )
```

time: 1780 us -> 1300 us (0.73)
  matrix products: 687 us -> 236 us
  Pallas kernels: 0 us -> 351 us
  local copies, waits for them, and re-layouts: 374 us -> 147 us
  other arithmetic: 296 us -> 126 us
  starting transfers between devices: 0.75 us -> 47.1 us
  blocking collectives: 39.6 us -> 0 us
  waiting for transfers between devices: 344 us -> 363 us
    pallas_call x0 -> x11, Pallas kernels: none -> 351 us  [the longest x3 152 us: attend_back(): pl.pallas_call(lambda *refs: attend_back_kernel(valid, *refs), grid=(clip...]
    dot_general x48 -> x3, matrix products: 363 us -> 13.1 us  [the longest x1 6.67 us: all_grads(): jnp.einsum('cvp,cpd->cvd', chosen_low, tubes, preferred_element_type=jnp....]
    ppermute x0 -> x67, waiting for transfers between devices: none -> 257 us  [the longest x27 211 us: rotate(): lax.ppermute(value, BOTH, [(i, i & ~6 | i + 2 & 6) for i in range(32)])]
    reduce_scatter x2 -> x0, waiting for transfers between devices: 251 us -> none  [scatter_group(): total = lax.psum_scatter(packed, ('row', 'col'), scatter_dimension=0)]
    convert_element_type x13 -> x14, other arithmetic: 132 us -> 11.2 us  [the longest x12 7.14 us: ring_reduce(): moved = rotate(total.astype(jnp.bfloat16)).astype(jnp.float32)]
    psum x1, waiting for transfers between devices: 0.01 us -> 106 us  [reduce_head(): return lax.psum(grad, BOTH)]
    all_gather x1 -> x0, waiting for transfers between devices: 93.1 us -> none  [gather_group(): everything = lax.all_gather(packed, ('row', 'col'), axis=0)]
    dot_general x28 -> x14, matrix products: 155 us -> 83.3 us  [product(): return jnp.dot(left, right, preferred_element_type=jnp.float32)]
  transfers between devices with their start and end apart: 4 -> 68, of which waited for: 3 -> 29; matrix products, arithmetic and copies ran while one was open for 20% -> 19% of each run, Pallas kernels for 0% -> 8%
where the time goes in v2:
time: 1300 us; the launch traced here: 1290 us
  waiting for transfers between devices  363 us (28%)
  Pallas kernels  351 us (27%)
  matrix products  236 us (18%)
  local copies, waits for them, and re-layouts  147 us (11%)
  other arithmetic  126 us (10%)
  starting transfers between devices  47.1 us (4%)
  between operations  18.8 us (1%)
    ppermute x27, waiting for transfers between devices, rotate(): lax.ppermute(value, BOTH, [(i, i & ~6 | i + 2 & 6) for i in range(32)])  211 us
    pallas_call x3, Pallas kernels, attend_back(): pl.pallas_call(lambda *refs: attend_back_kernel(valid, *refs), grid=(clip...  152 us
    psum x1, waiting for transfers between devices, reduce_head(): return lax.psum(grad, BOTH)  106 us
    pallas_call x3, Pallas kernels, attend(): pl.pallas_call(lambda *refs: attend_kernel(valid, *refs), grid=(clips, pa...  89.9 us
    dot_general x14, matrix products, product(): return jnp.dot(left, right, preferred_element_type=jnp.float32)  83.3 us
    dot_general x15, matrix products, product_right(): lax.dot_general(left, right, (((1,), (1,)), ((), ())), preferred_element_...  73.1 us
    dot_general x15, matrix products, product_left(): lax.dot_general(left, right, (((0,), (0,)), ((), ())), preferred_element_...  66.9 us
    pallas_call x3, Pallas kernels, unpack_chunk(): pl.pallas_call(lambda *refs: unpack_kernel(layout, *refs), grid=(32,), in...  62.1 us
  transfers between devices with their start and end apart: 68, of which 29 were waited for; matrix products, arithmetic and copies ran while one was open for 19% of the time, Pallas kernels for 8%

profile of v2, /device:TPU:0, one launch (start us, length us, event | category | flops | bytes accessed | tf_op | source)
XLA Modules:
  0.0 1289.4 jit_solution(11016672104270373795)
XLA Ops:
  65.2 29.7 %collective-permute-done.2 = bf16[1,276,768]{2,1,0:T(8,128)(2,1)} collective-permute-done((bf16[1,276,768]{2,1,0:T(8,128)(2,1)}, bf16[1,276,768]{2,1,0:T(8,128)(2,1)}, u32[]{:S(2)}, u32[]{:S(2)}) %collective-permute-start.2) | collective-permute-done | bytes 423968 | tf_op jit(solution)/shard_map/ppermute | solution.py:355
  117.8 31.9 %collective-permute-done.22 = bf16[2,240,768]{2,1,0:T(8,128)(2,1)S(1)} collective-permute-done((bf16[2,240,768]{2,1,0:T(8,128)(2,1)}, bf16[2,240,768]{2,1,0:T(8,128)(2,1)S(1)}, u32[]{:S(2)}, u32[]{:S(2)}) %collective-permute-start.22) | collective-permute-done | bytes 737312 | tf_op jit(solution)/shard_map/ppermute | solution.py:355
  165.4 14.8 %collective-permute-done.17 = bf16[4,192,768]{2,1,0:T(8,128)(2,1)} collective-permute-done((bf16[4,192,768]{2,1,0:T(8,128)(2,1)}, bf16[4,192,768]{2,1,0:T(8,128)(2,1)}, u32[]{:S(2)}, u32[]{:S(2)}) %collective-permute-start.17) | collective-permute-done | bytes 1179680 | tf_op jit(solution)/shard_map/ppermute | solution.py:355
  236.4 20.0 %unpack_chunk.4 = (bf16[768,3072]{1,0:T(8,128)(2,1)}, bf16[768,3072]{1,0:T(8,128)(2,1)}) custom-call(bf16[32,192,768]{2,1,0:T(8,128)(2,1)} %constant_dynamic-update-slice_fusion.8.refs_0_), custom_call_target="tpu_custom_call" | custom-call | bytes 18874368 | tf_op jit(solution)/shard_map/unpack_chunk/pallas_call | solution.py:541
  257.9 21.3 %unpack_chunk.3 = (bf16[768,6144]{1,0:T(8,128)(2,1)}, bf16[768,1536]{1,0:T(8,128)(2,1)}, bf16[32,36,768]{2,1,0:T(8,128)(2,1)}) custom-call(bf16[32,276,768]{2,1,0:T(8,128)(2,1)} %copy_dynamic-update-slice_fusion.refs_0_), custom_call_target="tpu_custom_call" | custom-call | bytes 27131904 | tf_op jit(solution)/shard_map/unpack_chunk/pallas_call | solution.py:541
  321.9 20.8 %unpack_chunk.5 = (bf16[768,6144]{1,0:T(8,128)(2,1)}, bf16[384,3072]{1,0:T(8,128)(2,1)}) custom-call(bf16[32,240,768]{2,1,0:T(8,128)(2,1)} %constant_dynamic-update-slice_fusion.refs_0_), custom_call_target="tpu_custom_call" | custom-call | bytes 23592960 | tf_op jit(solution)/shard_map/unpack_chunk/pallas_call | solution.py:541
  391.1 69.1 %attend.5 = (bf16[3136,384]{1,0:T(8,128)(2,1)}, f32[3136,384]{1,0:T(8,128)}) custom-call(bf16[3136,1152]{1,0:T(8,128)(2,1)} %convolution_convert_fusion.refs_0_.refs_1_.refs_2_, bf16[3136,1152]{1,0:T(8,128)(2,1)} %convolution_convert_fusion.refs_0_.refs_1_.refs_2_, bf16[3136,1152]{1,0:T(8,128)(2,1)} %convolution_convert_fusion.refs_0_.refs_1_.refs_2_), custom_call_target="tpu_custom_call" | custom-call | flops 30211571712 | bytes 14450688 | tf_op jit(solution)/shard_map/attend/pallas_call | solution.py:148
  487.9 12.1 multiply_reduce_fusion
  500.1 12.4 fusion.28
  512.5 16.5 %multiply_reduce_fusion.2 = (f32[384]{0:T(512)}, f32[3136]{0:T(1024)S(1)}, f32[3136,384]{1,0:T(8,128)S(1)}) fusion(f32[3136,384]{1,0:T(8,128)} %copy-done.4, f32[3136]{0:T(1024)S(1)} %fusion.82, f32[3136]{0:T(1024)S(1)} %broadcast_multiply_fusion, f32[384]{0:T(512)S(1)} %get-tuple-element.161, f32[384,1536]{1,0:T(8,128)S(1)} %copy-done.14, ...), kind=kOutput, calls=%fused_computation.36 | convolution fusion | flops 3718025728 | bytes 31301376 | tf_op jit(solution)/shard_map/dot_general | solution.py:42
  531.9 14.9 %multiply_convert_fusion = bf16[3136,1536]{1,0:T(8,128)(2,1)S(1)} fusion(f32[3136,1536]{1,0:T(8,128)} %get-tuple-element.195, bf16[384,2304]{1,0:T(8,128)(2,1)S(1)} %copy-done.34, f32[3136,384]{1,0:T(8,128)S(1)} %get-tuple-element.132, f32[3136]{0:T(1024)S(1)} %negate_multiply_fusion.2), kind=kOutput, calls=%fused_computation.10 | convolution fusion | flops 3759587328 | bytes 34914304 | tf_op jit(solution)/shard_map/dot_general | solution.py:32
  556.1 11.3 multiply_reduce_fusion.3
  576.6 126.0 %attend_back.3 = (bf16[3136,384]{1,0:T(8,128)(2,1)}, bf16[3136,384]{1,0:T(8,128)(2,1)}, bf16[3136,384]{1,0:T(8,128)(2,1)}) custom-call(bf16[3136,1152]{1,0:T(8,128)(2,1)} %convolution_convert_fusion.refs_0_.refs_1_.refs_2_, bf16[3136,1152]{1,0:T(8,128)(2,1)} %convolution_convert_fusion.refs_0_.refs_1_.refs_2_, ...), custom_call_target="tpu_custom_call" | custom-call | flops 75528929280 | bytes 24084480 | tf_op jit(solution)/shard_map/attend_back/pallas_call | solution.py:178
  738.0 10.5 convolution_convert_fusion.12
  748.6 105.9 %all-reduce.2.cloned.1.call-done = f32[384,1536]{1,0:T(8,128)} async-done(((f32[384,1536]{1,0:T(8,128)}), f32[384,1536]{1,0:T(8,128)}) %all-reduce.2.cloned.1.call-update) | async-done | bytes 2359312 | tf_op jit(solution)/shard_map/psum | solution.py:730
  874.7 13.2 %attend_back.4 = (bf16[320,768]{1,0:T(8,128)(2,1)}, bf16[320,768]{1,0:T(8,128)(2,1)}, bf16[320,768]{1,0:T(8,128)(2,1)}) custom-call(bf16[320,2304]{1,0:T(8,128)(2,1)} %convolution_convert_fusion.8.refs_0_.refs_1_.refs_2_, bf16[320,2304]{1,0:T(8,128)(2,1)} %convolution_convert_fusion.8.refs_0_.refs_1_.refs_2_, ...), custom_call_target="tpu_custom_call" | custom-call | flops 1572864000 | bytes 4915200 | tf_op jit(solution)/shard_map/attend_back/pallas_call | solution.py:178
  906.2 13.0 %attend_back.5 = (bf16[320,768]{1,0:T(8,128)(2,1)}, bf16[320,768]{1,0:T(8,128)(2,1)}, bf16[320,768]{1,0:T(8,128)(2,1)}) custom-call(bf16[320,2304]{1,0:T(8,128)(2,1)} %convolution_convert_fusion.9.refs_0_.refs_1_.refs_2_, bf16[320,2304]{1,0:T(8,128)(2,1)} %convolution_convert_fusion.9.refs_0_.refs_1_.refs_2_, ...), custom_call_target="tpu_custom_call" | custom-call | flops 1572864000 | bytes 4915200 | tf_op jit(solution)/shard_map/attend_back/pallas_call | solution.py:178
  967.2 23.3 %pack_chunks.3 = (bf16[32,144,768]{2,1,0:T(8,128)(2,1)}, bf16[32,132,768]{2,1,0:T(8,128)(2,1)}, bf16[32,96,768]{2,1,0:T(8,128)(2,1)}) custom-call(bf16[768,2304]{1,0:T(8,128)(2,1)} %convolution_convert_fusion.2.refs_0_, bf16[768,768]{1,0:T(8,128)(2,1)} %convolution_convert_fusion.15.refs_1_, bf16[768,3072]{1,0:T(8,128)(2,1)} %convolution_convert_fusion.5.refs_2_, ...), custom_call_target="tpu_custom_call" | custom-call | bytes 36569088 | tf_op jit(solution)/shard_map/pack_chunks/pallas_call | solution.py:607
  999.0 23.3 %pack_chunks.2 = (bf16[32,144,768]{2,1,0:T(8,128)(2,1)}, bf16[32,96,768]{2,1,0:T(8,128)(2,1)}, bf16[32,96,768]{2,1,0:T(8,128)(2,1)}) custom-call(bf16[768,2304]{1,0:T(8,128)(2,1)} %convolution_convert_fusion.3.refs_0_, bf16[768,768]{1,0:T(8,128)(2,1)} %convolution_convert_fusion.16.refs_1_, bf16[768,3072]{1,0:T(8,128)(2,1)} %convolution_convert_fusion.7.refs_2_, ...), custom_call_target="tpu_custom_call" | custom-call | bytes 33030144 | tf_op jit(solution)/shard_map/pack_chunks/pallas_call | solution.py:607
  1074.5 10.4 collective-permute-done.56
  1118.5 14.6 %collective-permute-done.33 = bf16[2,96,768]{2,1,0:T(8,128)(2,1)S(1)} collective-permute-done((bf16[2,96,768]{2,1,0:T(8,128)(2,1)S(1)}, bf16[2,96,768]{2,1,0:T(8,128)(2,1)S(1)}, u32[]{:S(2)}, u32[]{:S(2)}) %collective-permute-start.33) | collective-permute-done | bytes 294944 | tf_op jit(solution)/shard_map/ppermute | solution.py:355
  1134.7 16.4 %collective-permute-done.58 = bf16[4,96,768]{2,1,0:T(8,128)(2,1)S(1)} collective-permute-done((bf16[4,96,768]{2,1,0:T(8,128)(2,1)S(1)}, bf16[4,96,768]{2,1,0:T(8,128)(2,1)S(1)}, u32[]{:S(2)}, u32[]{:S(2)}) %collective-permute-start.58) | collective-permute-done | bytes 589856 | tf_op jit(solution)/shard_map/ppermute | solution.py:355
  1157.0 21.1 %collective-permute-done.65 = bf16[2,96,768]{2,1,0:T(8,128)(2,1)S(1)} collective-permute-done((bf16[2,96,768]{2,1,0:T(8,128)(2,1)S(1)}, bf16[2,96,768]{2,1,0:T(8,128)(2,1)S(1)}, u32[]{:S(2)}, u32[]{:S(2)}) %collective-permute-start.65) | collective-permute-done | bytes 294944 | tf_op jit(solution)/shard_map/ppermute | solution.py:351
  1216.0 11.0 collective-permute-done.52
  (808 shorter events, 607.1 us)
Async XLA Ops:
  7.2 847.3 %all-reduce.2.cloned.1.call-start = ((), (), s32[]{:S(2)}) async-start(), calls=%async_computation | async-start | bytes 4718592 | tf_op jit(solution)/shard_map/psum | solution.py:730
  43.5 55.3 %collective-permute-start.13 = (bf16[4,192,768]{2,1,0:T(8,128)(2,1)}, bf16[4,192,768]{2,1,0:T(8,128)(2,1)}, u32[]{:S(2)}, u32[]{:S(2)}) collective-permute-start(bf16[4,192,768]{2,1,0:T(8,128)(2,1)} %get-tuple-element.135), channel_id=1, source_target_pairs={{0,2},{1,3},{2,4},{3,5},{4,6},{5,7},{6,0},{7,1},{8,10},{9,11},{10,... | collective-permute-start | bytes 3538952 | tf_op jit(solution)/shard_map/ppermute | solution.py:355
  60.4 34.5 %collective-permute-start.2 = (bf16[1,276,768]{2,1,0:T(8,128)(2,1)}, bf16[1,276,768]{2,1,0:T(8,128)(2,1)}, u32[]{:S(2)}, u32[]{:S(2)}) collective-permute-start(bf16[1,276,768]{2,1,0:T(8,128)(2,1)} %collective-permute-done.1), channel_id=1, source_target_pairs={{0,2},{1,3},{2,4},{3,5},{4,6},{5,7},{6,0},{7,1},{8,10},{9,11},{10,... | collective-permute-start | bytes 1271816 | tf_op jit(solution)/shard_map/ppermute | solution.py:355
  60.5 53.9 %collective-permute-start.12 = (bf16[4,192,768]{2,1,0:T(8,128)(2,1)}, bf16[4,192,768]{2,1,0:T(8,128)(2,1)}, u32[]{:S(2)}, u32[]{:S(2)}) collective-permute-start(bf16[4,192,768]{2,1,0:T(8,128)(2,1)} %get-tuple-element.135), channel_id=1, source_target_pairs={{0,1},{1,0},{2,3},{3,2},{4,5},{5,4},{6,7},{7,6},{8,9},{9,8},{10,11... | collective-permute-start | bytes 3538952 | tf_op jit(solution)/shard_map/ppermute | solution.py:351
  61.7 49.0 %collective-permute-start.21 = (bf16[2,240,768]{2,1,0:T(8,128)(2,1)}, bf16[2,240,768]{2,1,0:T(8,128)(2,1)}, u32[]{:S(2)}, u32[]{:S(2)}) collective-permute-start(bf16[2,240,768]{2,1,0:T(8,128)(2,1)} %collective-permute-done.20), channel_id=1, source_target_pairs={{0,2},{1,3},{2,4},{3,5},{4,6},{5,7},{6,0},{7,1},{8,10},{9,11},{10,... | collective-permute-start | bytes 2211848 | tf_op jit(solution)/shard_map/ppermute | solution.py:355
  97.7 58.6 %collective-permute-start.6 = (bf16[4,276,768]{2,0,1:T(4,128)(2,1)}, bf16[4,276,768]{2,0,1:T(4,128)(2,1)}, u32[]{:S(2)}, u32[]{:S(2)}) collective-permute-start(bf16[4,276,768]{2,0,1:T(4,128)(2,1)} %copy.68), channel_id=1, source_target_pairs={{0,16},{1,17},{2,18},{3,19},{4,20},{5,21},{6,22},{7,23},{8,24},{9,... | collective-permute-start | bytes 5087240 | tf_op jit(solution)/shard_map/ppermute | solution.py:351
  98.8 50.9 %collective-permute-start.15 = (bf16[4,192,768]{2,1,0:T(8,128)(2,1)}, bf16[4,192,768]{2,1,0:T(8,128)(2,1)}, u32[]{:S(2)}, u32[]{:S(2)}) collective-permute-start(bf16[4,192,768]{2,1,0:T(8,128)(2,1)} %collective-permute-done.13), channel_id=1, source_target_pairs={{0,2},{1,3},{2,4},{3,5},{4,6},{5,7},{6,0},{7,1},{8,10},{9,11},{10,... | collective-permute-start | bytes 3538952 | tf_op jit(solution)/shard_map/ppermute | solution.py:355
  110.7 39.0 %collective-permute-start.22 = (bf16[2,240,768]{2,1,0:T(8,128)(2,1)}, bf16[2,240,768]{2,1,0:T(8,128)(2,1)S(1)}, u32[]{:S(2)}, u32[]{:S(2)}) collective-permute-start(bf16[2,240,768]{2,1,0:T(8,128)(2,1)} %collective-permute-done.21), channel_id=1, source_target_pairs={{0,2},{1,3},{2,4},{3,5},{4,6},{5,7},{6,0},{7,1},{8,10},{9,11},{10,... | collective-permute-start | bytes 2211848 | tf_op jit(solution)/shard_map/ppermute | solution.py:355
  113.8 48.1 %collective-permute-start.4 = (bf16[4,276,768]{2,0,1:T(4,128)(2,1)}, bf16[4,276,768]{2,0,1:T(4,128)(2,1)}, u32[]{:S(2)}, u32[]{:S(2)}) collective-permute-start(bf16[4,276,768]{2,0,1:T(4,128)(2,1)} %copy.68), channel_id=1, source_target_pairs={{0,8},{1,9},{2,10},{3,11},{4,12},{5,13},{6,14},{7,15},{8,0},{9,1},... | collective-permute-start | bytes 5087240 | tf_op jit(solution)/shard_map/ppermute | solution.py:351
  114.3 48.1 %collective-permute-start.3 = (bf16[4,276,768]{2,0,1:T(4,128)(2,1)}, bf16[4,276,768]{2,0,1:T(4,128)(2,1)S(1)}, u32[]{:S(2)}, u32[]{:S(2)}) collective-permute-start(bf16[4,276,768]{2,0,1:T(4,128)(2,1)} %copy.68), channel_id=1, source_target_pairs={{0,1},{1,0},{2,3},{3,2},{4,5},{5,4},{6,7},{7,6},{8,9},{9,8},{10,11... | collective-permute-start | bytes 5087240 | tf_op jit(solution)/shard_map/ppermute | solution.py:351
  156.4 44.4 %collective-permute-start.16 = (bf16[4,192,768]{2,1,0:T(8,128)(2,1)}, bf16[4,192,768]{2,1,0:T(8,128)(2,1)}, u32[]{:S(2)}, u32[]{:S(2)}) collective-permute-start(bf16[4,192,768]{2,1,0:T(8,128)(2,1)} %collective-permute-done.15), channel_id=1, source_target_pairs={{0,1},{1,0},{2,3},{3,2},{4,5},{5,4},{6,7},{7,6},{8,9},{9,8},{10,11... | collective-permute-start | bytes 3538952 | tf_op jit(solution)/shard_map/ppermute | solution.py:351
  161.9 66.1 %collective-permute-start.24 = (bf16[8,240,768]{2,1,0:T(8,128)(2,1)}, bf16[8,240,768]{2,1,0:T(8,128)(2,1)}, u32[]{:S(2)}, u32[]{:S(2)}) collective-permute-start(bf16[8,240,768]{2,1,0:T(8,128)(2,1)} %constant_dynamic-update-slice_fusion.4), channel_id=1, source_target_pairs={{0,8},{1,9},{2,10},{3,11},{4,12},{5,13},{6,14},{7,15},{8,0},{9,1},... | collective-permute-start | bytes 8847368 | tf_op jit(solution)/shard_map/ppermute | solution.py:351
  162.4 65.6 %collective-permute-start.23 = (bf16[8,240,768]{2,1,0:T(8,128)(2,1)}, bf16[8,240,768]{2,1,0:T(8,128)(2,1)}, u32[]{:S(2)}, u32[]{:S(2)}) collective-permute-start(bf16[8,240,768]{2,1,0:T(8,128)(2,1)} %constant_dynamic-update-slice_fusion.4), channel_id=1, source_target_pairs={{0,1},{1,0},{2,3},{3,2},{4,5},{5,4},{6,7},{7,6},{8,9},{9,8},{10,11... | collective-permute-start | bytes 8847368 | tf_op jit(solution)/shard_map/ppermute | solution.py:351
  164.6 49.4 %collective-permute-start.8 = (bf16[4,276,768]{2,0,1:T(4,128)(2,1)}, bf16[4,276,768]{2,0,1:T(4,128)(2,1)S(1)}, u32[]{:S(2)}, u32[]{:S(2)}) collective-permute-start(bf16[4,276,768]{2,0,1:T(4,128)(2,1)} %collective-permute-done.4), channel_id=1, source_target_pairs={{0,16},{1,17},{2,18},{3,19},{4,20},{5,21},{6,22},{7,23},{8,24},{9,... | collective-permute-start | bytes 5087240 | tf_op jit(solution)/shard_map/ppermute | solution.py:351
  214.0 42.5 %collective-permute-start.9 = (bf16[4,276,768]{2,0,1:T(4,128)(2,1)S(1)}, bf16[4,276,768]{2,0,1:T(4,128)(2,1)S(1)}, u32[]{:S(2)}, u32[]{:S(2)}) collective-permute-start(bf16[4,276,768]{2,0,1:T(4,128)(2,1)S(1)} %collective-permute-done.8), channel_id=1, source_target_pairs={{0,1},{1,0},{2,3},{3,2},{4,5},{5,4},{6,7},{7,6},{8,9},{9,8},{10,11... | collective-permute-start | bytes 5087240 | tf_op jit(solution)/shard_map/ppermute | solution.py:351
  228.0 90.3 %collective-permute-start.25 = (bf16[8,240,768]{2,1,0:T(8,128)(2,1)}, bf16[8,240,768]{2,1,0:T(8,128)(2,1)}, u32[]{:S(2)}, u32[]{:S(2)}) collective-permute-start(bf16[8,240,768]{2,1,0:T(8,128)(2,1)} %collective-permute-done.24), channel_id=1, source_target_pairs={{0,1},{1,0},{2,3},{3,2},{4,5},{5,4},{6,7},{7,6},{8,9},{9,8},{10,11... | collective-permute-start | bytes 8847368 | tf_op jit(solution)/shard_map/ppermute | solution.py:351
  967.1 55.3 %collective-permute-start.26 = (f32[5377]{0:T(1024)S(1)}, f32[5377]{0:T(1024)S(1)}, u32[]{:S(2)}, u32[]{:S(2)}) collective-permute-start(f32[5377]{0:T(1024)S(1)} %concatenate.73), channel_id=1, source_target_pairs={{0,1},{1,0},{2,3},{3,2},{4,5},{5,4},{6,7},{7,6},{8,9},{9,8},{10,11... | collective-permute-start | bytes 64532 | tf_op jit(solution)/shard_map/ppermute | solution.py:351
  993.8 57.7 %collective-permute-start.61 = (bf16[16,96,768]{2,1,0:T(8,128)(2,1)}, bf16[16,96,768]{2,1,0:T(8,128)(2,1)}, u32[]{:S(2)}, u32[]{:S(2)}) collective-permute-start(bf16[16,96,768]{2,1,0:T(8,128)(2,1)} %constant_dynamic-slice_fusion), channel_id=1, source_target_pairs={{0,1},{1,0},{2,3},{3,2},{4,5},{5,4},{6,7},{7,6},{8,9},{9,8},{10,11... | collective-permute-start | bytes 7077896 | tf_op jit(solution)/shard_map/ppermute | solution.py:351
  1037.9 47.9 %collective-permute-start.49 = (bf16[16,132,768]{2,0,1:T(8,128)(2,1)}, bf16[16,132,768]{2,0,1:T(8,128)(2,1)S(1)}, u32[]{:S(2)}, u32[]{:S(2)}) collective-permute-start(bf16[16,132,768]{2,0,1:T(8,128)(2,1)} %copy.81), channel_id=1, source_target_pairs={{0,1},{1,0},{2,3},{3,2},{4,5},{5,4},{6,7},{7,6},{8,9},{9,8},{10,11... | collective-permute-start | bytes 9732104 | tf_op jit(solution)/shard_map/ppermute | solution.py:351
  1041.8 47.2 %collective-permute-start.43 = (bf16[16,144,768]{2,1,0:T(8,128)(2,1)}, bf16[16,144,768]{2,1,0:T(8,128)(2,1)}, u32[]{:S(2)}, u32[]{:S(2)}) collective-permute-start(bf16[16,144,768]{2,1,0:T(8,128)(2,1)} %constant_dynamic-slice_fusion.3), channel_id=1, source_target_pairs={{0,1},{1,0},{2,3},{3,2},{4,5},{5,4},{6,7},{7,6},{8,9},{9,8},{10,11... | collective-permute-start | bytes 10616840 | tf_op jit(solution)/shard_map/ppermute | solution.py:351
  1051.5 40.8 %collective-permute-start.37 = (bf16[16,144,768]{2,1,0:T(8,128)(2,1)}, bf16[16,144,768]{2,1,0:T(8,128)(2,1)}, u32[]{:S(2)}, u32[]{:S(2)}) collective-permute-start(bf16[16,144,768]{2,1,0:T(8,128)(2,1)} %constant_dynamic-slice_fusion.4), channel_id=1, source_target_pairs={{0,1},{1,0},{2,3},{3,2},{4,5},{5,4},{6,7},{7,6},{8,9},{9,8},{10,11... | collective-permute-start | bytes 10616840 | tf_op jit(solution)/shard_map/ppermute | solution.py:351
  1089.0 110.0 %collective-permute-start.50 = (bf16[8,132,768]{2,0,1:T(8,128)(2,1)}, bf16[8,132,768]{2,0,1:T(8,128)(2,1)}, u32[]{:S(2)}, u32[]{:S(2)}) collective-permute-start(bf16[8,132,768]{2,0,1:T(8,128)(2,1)} %copy.83), channel_id=1, source_target_pairs={{0,8},{1,9},{2,10},{3,11},{4,12},{5,13},{6,14},{7,15},{8,0},{9,1},... | collective-permute-start | bytes 4866056 | tf_op jit(solution)/shard_map/ppermute | solution.py:351
  1092.3 121.2 %collective-permute-start.44 = (bf16[8,144,768]{2,1,0:T(8,128)(2,1)S(1)}, bf16[8,144,768]{2,1,0:T(8,128)(2,1)}, u32[]{:S(2)}, u32[]{:S(2)}) collective-permute-start(bf16[8,144,768]{2,1,0:T(8,128)(2,1)S(1)} %dynamic-slice_convert_fusion), channel_id=1, source_target_pairs={{0,16},{1,17},{2,18},{3,19},{4,20},{5,21},{6,22},{7,23},{8,24},{9,... | collective-permute-start | bytes 5308424 | tf_op jit(solution)/shard_map/ppermute | solution.py:351
  1115.8 111.3 %collective-permute-start.38 = (bf16[8,144,768]{2,1,0:T(8,128)(2,1)S(1)}, bf16[8,144,768]{2,1,0:T(8,128)(2,1)}, u32[]{:S(2)}, u32[]{:S(2)}) collective-permute-start(bf16[8,144,768]{2,1,0:T(8,128)(2,1)S(1)} %dynamic-slice_convert_fusion.1), channel_id=1, source_target_pairs={{0,16},{1,17},{2,18},{3,19},{4,20},{5,21},{6,22},{7,23},{8,24},{9,... | collective-permute-start | bytes 5308424 | tf_op jit(solution)/shard_map/ppermute | solution.py:351
  (240 other events, 4523.8 us)
Sparse Core Ops, SparseCore 0:
  718.9 135.5 all-reduce.1
